TPU v7x, 256 devices: a whole 4x4x8 slice. The times are simulated.
256 devices in a mesh: rep: 16 (over z, y_hi), exp: 16 (over y_lo, x, core).
Axes of the slice: x: 4, y: 4 (y_hi: 2, y_lo: 2; y = y_hi * 2 + y_lo), z: 8, core: 2. Of those that a mesh axis runs over, the one named last changes fastest.
Arguments:
- tokens: bfloat16 [8192, 2048], P(('rep', 'exp')), may hold values from -6 to 6
- attend_weight: bfloat16 [2048, 16, 256], P(None, 'exp'), may hold values from -0.125 to 0.125
- value_weight: bfloat16 [2048, 32, 256], P(None, 'exp'), may hold values from -0.125 to 0.125
- rate_weight: bfloat16 [2048, 32, 2], P(None, 'exp'), may hold values from -0.125 to 0.125
- decay_rate: float32 [32], P('exp'), may hold values from 0.002 to 0.2
- output_weight: bfloat16 [32, 128, 2048], P('exp'), may hold values from -0.09375 to 0.09375
- state_cache: float32 [128, 32, 128, 128], P('rep', 'exp'), may hold values from -2.4 to 2.4
- resume_from: int32 [128], replicated, may hold values from 0 to 127, as said below
- expert_index: int32 [8192, 10], P(('rep', 'exp')), may hold values from 0 to 15, all different within a row; in each aligned block of 32 rows (0 to 31, 32 to 63, ...) at most 32 rows name the same one
- route_weight: float32 [8192, 10], P(('rep', 'exp')), may hold values from 0.02 to 0.3
- expert_inner: bfloat16 [16, 2048, 1024], P('exp'), may hold values from -0.125 to 0.125
- expert_outer: bfloat16 [16, 512, 2048], P('exp'), may hold values from -0.25 to 0.25
Outputs:
- layer_output: bfloat16 [8192, 2048], P(('rep', 'exp'))
- final_state: float32 [128, 32, 128, 128], P('rep', 'exp')
Inputs may be any that keep to these rules, and one draw needn't show every extreme that they name: `resume_from`: entry r * 8 + b is the cache row of trajectory b of group r; cache row c belongs to group c // 8. The 8 trajectories of one group take their rows from 8 different groups; a row may serve several groups. `expert_index`: each row names 10 different experts.
All inputs are finite; a program needn't handle non-finite values.
Results may differ from a plain program's by a relative error of at most 0.013.
Values may be sent and summed in bfloat16 or wider, within the bound.
No kernel may reach another device: no remote copies, remote signals or barrier semaphores. Data moves between devices by JAX's collectives and lax.ppermute only.
A program may use at most 128 MiB of HBM per device.

v0:
```python
import jax
import jax.numpy as jnp
from jax import lax
from jax.experimental import pallas as pl
from jax.experimental.pallas import tpu as pltpu
from jax.sharding import PartitionSpec as P


EPSILON = 1e-06
F32 = jnp.float32
BF16 = jnp.bfloat16

NY, NX, NC = 2, 4, 2


def place(y, x, c):
    return (y * NX + x) * NC + c


SWAP = [(i, i ^ 1) for i in range(NY * NX * NC)]


def spread(dx):
    return [
        (place(y, x, c), place(y ^ c, (x + dx) % NX, y))
        for y in range(NY)
        for x in range(NX)
        for c in range(NC)
    ]


def collect(dx):
    return [(b, a) for a, b in spread(dx)]


def on_chip(values):
    return pltpu.with_memory_space_constraint(values, pltpu.VMEM)


def rms_scale(values):
    return values * lax.rsqrt(jnp.mean(values * values, axis=-1, keepdims=True) + EPSILON)


def halves(values):
    high = values.astype(BF16)
    return high, (values - high.astype(F32)).astype(BF16)


def left(values):
    high, low = halves(values)
    return jnp.concatenate([high, low, high], axis=1)


def right(values, axis=0):
    high, low = halves(values)
    return jnp.concatenate([high, high, low], axis=axis)


def dot(a, b, dims=((1,), (0,))):
    return lax.dot_general(a, b, (dims, ((), ())), preferred_element_type=F32)


def send_kernel(resume_ref, cache_ref, out_ref, short_ref, sems):
    trajs, slots = cache_ref.shape[0], out_ref.shape[0]
    me = lax.axis_index("rep")
    for row in range(trajs):
        short_ref[row] = cache_ref[row].astype(BF16)
    copies = []
    for slot in range(slots):
        row = jnp.int32(0)
        for place_of in range(trajs):
            value = resume_ref[slot * trajs + place_of]
            row = jnp.where(value // trajs == me, value % trajs, row)
        copies.append(pltpu.make_async_copy(short_ref.at[row], out_ref.at[slot], sems.at[slot]))
        copies[-1].start()
    for copy in copies:
        copy.wait()


def chunk_kernel(
    decay_own_ref, decay_other_ref, first_ref, second_ref, third_ref, fourth_ref, attend_own_ref, value_own_ref, rate_own_ref,
    attend_other_ref, value_other_ref, rate_other_ref,
    mix_ref, base_ref, key_ref, close_ref, gate_ref, proj_ref, rate_ref,
):
    width = 64
    row = lax.broadcasted_iota(jnp.int32, (width, width), 0)
    col = lax.broadcasted_iota(jnp.int32, (width, width), 1)
    row3 = lax.broadcasted_iota(jnp.int32, (width, 3 * width), 0)
    col3 = lax.broadcasted_iota(jnp.int32, (width, 3 * width), 1) % width
    lower3 = (col3 <= row3).astype(F32).astype(BF16)
    eye = (col == row).astype(F32)
    lane = lax.broadcasted_iota(jnp.int32, (1, 128), 1)
    decays = [
        jnp.where(lane == 0, ref[0], jnp.where(lane == 2, ref[1], 0.0))
        for ref in (decay_own_ref, decay_other_ref)
    ]
    normed = jnp.concatenate(
        [
            rms_scale(ref[...].astype(F32)).astype(BF16)
            for ref in (first_ref, second_ref, third_ref, fourth_ref)
        ],
        axis=0,
    )
    weights = (
        (attend_own_ref, value_own_ref, rate_own_ref),
        (attend_other_ref, value_other_ref, rate_other_ref),
    )
    for part, (attend, value, rate) in enumerate(weights):
        proj_ref[part, :, 0:256] = dot(normed, attend[...])
        for head in range(2):
            both_parts = dot(normed, value[head])
            proj_ref[part, :, 256 + 128 * head : 384 + 128 * head] = both_parts[:, :128]
            unit = 2 * part + head
            gate_ref[:, unit * 128 : (unit + 1) * 128] = both_parts[:, 128:]
        padded = jnp.concatenate([rate[...], jnp.zeros((120, rate.shape[1]), BF16)], axis=0)
        rate_ref[part] = dot(normed, padded, ((1,), (1,)))
    for pair in range(2):
        units = []
        for traj in (2 * pair, 2 * pair + 1):
            span = slice(width * traj, width * (traj + 1))
            for part in range(2):
                query = proj_ref[part, span, 0:128]
                query = query * lax.rsqrt(jnp.sum(query * query, axis=-1, keepdims=True) + EPSILON)
                query = query * (128 ** (-0.5))
                key = proj_ref[part, span, 128:256]
                key = key * lax.rsqrt(jnp.sum(key * key, axis=-1, keepdims=True) + EPSILON)
                rates = rate_ref[part, span, :]
                plus = jnp.maximum(rates, 0.0) + jnp.log1p(jnp.exp(-jnp.abs(rates)))
                log_decay = -decays[part] * plus
                strength = jax.nn.sigmoid(rates)
                high, rest = halves(log_decay)
                low = (log_decay - high.astype(F32) - rest.astype(F32)).astype(BF16)
                summed = dot(lower3, jnp.concatenate([high, rest, low], axis=0))
                summed_rows = jnp.transpose(summed)
                products = dot(
                    left(jnp.concatenate([key, query], axis=0)), right(key, axis=1), ((1,), (1,))
                )
                for head in range(2):
                    values = proj_ref[part, span, 256 + 128 * head : 384 + 128 * head]
                    s_col = summed[:, 2 * head : 2 * head + 1]
                    s_row = summed_rows[2 * head : 2 * head + 1, :]
                    beta = strength[:, 2 * head + 1 : 2 * head + 2]
                    ratio = jnp.where(col <= row, jnp.exp(jnp.minimum(s_col - s_row, 0.0)), 0.0)
                    below = jnp.where(col < row, beta * ratio * products[:width], 0.0)
                    grown = jnp.exp(s_col)
                    units.append(
                        dict(
                            at=(traj, 2 * part + head),
                            key=key,
                            query=query,
                            s=s_col,
                            grown=grown,
                            weights=ratio * products[width:],
                            below=below,
                            below3=left(below),
                            side=jnp.concatenate([beta * values, (beta * grown) * key], axis=1),
                        )
                    )
        size = 1
        while size < width:
            corner = ((row // size) % 2 == 1) & (row // size == col // size + 1)
            corner3 = ((row3 // size) % 2 == 1) & (row3 // size == col3 // size + 1)
            if size == 1:
                for unit in units:
                    unit["inverse"] = eye - jnp.where(corner, unit["below"], 0.0)
            else:
                for unit in units:
                    step = jnp.where(corner3, unit["below3"], jnp.zeros_like(unit["below3"]))
                    unit["middle"] = dot(step, right(unit["inverse"]))
                for unit in units:
                    unit["inverse"] = unit["inverse"] - dot(
                        left(unit["inverse"]), right(unit["middle"])
                    )
            size *= 2
        for unit in units:
            unit["update"] = dot(left(unit["inverse"]), right(unit["side"]))
        for unit in units:
            traj, number = unit["at"]
            update, key, grown, s_col = unit["update"], unit["key"], unit["grown"], unit["s"]
            seen = dot(left(unit["weights"]), right(update))
            mix_ref[traj, number, 0:width, :] = update[:, 128:]
            mix_ref[traj, number, width:, :] = grown * unit["query"] - seen[:, 128:]
            base_ref[traj, number, 0:width, :] = update[:, :128]
            base_ref[traj, number, width:, :] = seen[:, :128]
            closing = s_col[width - 1 : width, :]
            key_ref[traj, number] = jnp.exp(closing - s_col) * key
            close_ref[traj, number] = jnp.broadcast_to(jnp.exp(closing), (1, 128))


def state_kernel(
    resume_ref, spot_ref, gate_ref, mix_ref, base_ref, key_ref, close_ref, held_ref, sent_ref, out_own_ref,
    out_other_ref, first_ref, second_ref, third_ref, fourth_ref, keep_ref, give_ref, gated_ref,
):
    width = 64
    for traj in range(4):
        span = slice(width * traj, width * (traj + 1))
        to_place = (spot_ref[2] + 4 - traj) % 4
        from_slot = resume_ref[spot_ref[0] * 8 + spot_ref[1] * 4 + to_place] // 8
        for part in range(2):
            for head in range(2):
                unit = part * 2 + head
                state = held_ref[from_slot, head] if part == 0 else sent_ref[from_slot, head]
                high, low = halves(mix_ref[traj, unit])
                mixed = dot(
                    jnp.concatenate([high, low], axis=1),
                    jnp.concatenate([state, state], axis=1),
                    ((1,), (1,)),
                )
                update = base_ref[traj, unit, 0:width, :] - mixed[:width]
                read = base_ref[traj, unit, width:, :] + mixed[width:]
                high, low = halves(update)
                final = close_ref[traj, unit] * state.astype(F32) + dot(
                    jnp.concatenate([high, low, high], axis=0), right(key_ref[traj, unit]), ((0,), (0,))
                )
                (keep_ref if part == 0 else give_ref)[to_place, head] = final
                gate = gate_ref[span, 128 * unit : 128 * (unit + 1)]
                gated_ref[span, 128 * unit : 128 * (unit + 1)] = (
                    rms_scale(read) * (gate * jax.nn.sigmoid(gate))
                ).astype(BF16)
    partial = (
        dot(gated_ref[:, 0:256], out_own_ref[...]) + dot(gated_ref[:, 256:512], out_other_ref[...])
    ).astype(BF16)
    for traj, ref in enumerate((first_ref, second_ref, third_ref, fourth_ref)):
        ref[...] = partial[width * traj : width * (traj + 1)]


def expert_kernel(
    mine_ref, first_ref, second_ref, third_ref, fourth_ref, share_ref, inner_own_ref, outer_own_ref,
    inner_other_ref, outer_other_ref, *rest,
):
    *out_refs, inner_ref, outer_ref, sems = rest
    fetches = [
        pltpu.make_async_copy(inner_own_ref, inner_ref, sems.at[0]),
        pltpu.make_async_copy(outer_own_ref, outer_ref, sems.at[1]),
    ]
    for fetch in fetches:
        fetch.start()
    rows = jnp.concatenate(
        [first_ref[...], second_ref[...], third_ref[...], fourth_ref[...]], axis=0
    )
    column = lax.broadcasted_iota(jnp.int32, share_ref.shape, 1)
    total = None
    for number, inner, outer in (
        (mine_ref[0] ^ 1, inner_other_ref, outer_other_ref),
        (mine_ref[0], inner_ref, outer_ref),
    ):
        if total is not None:
            fetches[0].wait()
        half = outer.shape[0]
        gate = dot(rows, inner[:, :half])
        up = dot(rows, inner[:, half:])
        activated = (gate * jax.nn.sigmoid(gate) * up).astype(BF16)
        if total is not None:
            fetches[1].wait()
        produced = dot(activated, outer[...]).astype(BF16).astype(F32)
        weight = jnp.sum(jnp.where(column == number, share_ref[...], 0.0), axis=1, keepdims=True)
        total = weight * produced if total is None else total + weight * produced
    for number, ref in enumerate(out_refs):
        ref[...] = total[64 * number : 64 * (number + 1)].astype(BF16)


def local(
    tokens,
    attend_weight,
    value_weight,
    rate_weight,
    decay_rate,
    output_weight,
    state_cache,
    resume_from,
    expert_index,
    route_weight,
    expert_inner,
    expert_outer,
):
    rows, model = tokens.shape
    both = 2 * rows
    trajs = state_cache.shape[0]
    groups = lax.axis_size("rep")
    me = lax.axis_index("rep")
    mine = lax.axis_index("exp")
    my_core = mine % NC
    my_x = (mine // NC) % NX
    first = my_core == 0

    def swap(values):
        return lax.ppermute(values, "exp", SWAP)

    def in_order(own, other):
        return jnp.where(
            first, jnp.concatenate([own, other], axis=0), jnp.concatenate([other, own], axis=0)
        )

    def spread_all(values):
        return [lax.ppermute(values, "exp", spread(dx)) for dx in range(NX)]

    spot = jnp.stack([me, my_core, my_x]).astype(jnp.int32)

    heads, dv, dk = state_cache.shape[1:]
    slots = pl.pallas_call(
        send_kernel,
        in_specs=[pl.BlockSpec(memory_space=pltpu.SMEM), pl.BlockSpec(memory_space=pltpu.VMEM)],
        out_specs=pl.BlockSpec(memory_space=pl.ANY),
        out_shape=jax.ShapeDtypeStruct((groups, heads, dv, dk), BF16),
        scratch_shapes=[
            pltpu.VMEM((trajs, heads, dv, dk), BF16),
            pltpu.SemaphoreType.DMA((groups,)),
        ],
    )(resume_from, state_cache)

    tokens_other, slots = lax.optimization_barrier((swap(tokens), slots))
    arrived = lax.all_to_all(slots, "rep", split_axis=0, concat_axis=0, tiled=True)
    token_rows = in_order(tokens, tokens_other)
    pieces = []
    for dx in range(NX):
        pieces.append(lax.ppermute(token_rows, "exp", spread(dx)))

    attend_own = attend_weight.reshape(model, -1)
    rate_own = jnp.pad(jnp.transpose(rate_weight, (1, 2, 0)).reshape(2 * heads, model), ((0, 4), (0, 0)))
    rate_other = swap(rate_own)
    decay_other = swap(decay_rate)
    attend_other = swap(attend_own)
    token_rows, value_weight = lax.optimization_barrier((token_rows, value_weight))
    value_own = jnp.transpose(value_weight, (1, 0, 2))
    value_other = swap(value_own)
    out_own = output_weight.reshape(-1, model)
    inner_own, outer_own = expert_inner[0], expert_outer[0]
    experts = lax.axis_size("exp")
    share = jnp.sum(
        jnp.where(
            expert_index[:, :, None] == jnp.arange(experts, dtype=jnp.int32), route_weight[:, :, None], 0.0
        ),
        axis=1,
    )
    share = jnp.pad(share, ((0, 0), (0, 128 - experts)))
    share_other = swap(share)
    shares = jnp.concatenate(spread_all(in_order(share, share_other)), axis=0)

    *pieces, shares, rate_other, decay_other, out_sent, inner_sent, outer_sent = (
        lax.optimization_barrier(
            (*pieces, shares, rate_other, decay_other, out_own, inner_own, outer_own)
        )
    )
    out_other, inner_other, outer_other = swap(out_sent), swap(inner_sent), swap(outer_sent)

    vmem = pl.BlockSpec(memory_space=pltpu.VMEM)
    smem = pl.BlockSpec(memory_space=pltpu.SMEM)
    mix, base, keys, close, gates = pl.pallas_call(
        chunk_kernel,
        in_specs=[smem] * 2 + [vmem] * 10,
        out_specs=[vmem] * 5,
        out_shape=[
            jax.ShapeDtypeStruct((NX, 4, 128, 128), F32),
            jax.ShapeDtypeStruct((NX, 4, 128, 128), F32),
            jax.ShapeDtypeStruct((NX, 4, 64, 128), F32),
            jax.ShapeDtypeStruct((NX, 4, 1, 128), F32),
            jax.ShapeDtypeStruct((NX * both, 512), F32),
        ],
        scratch_shapes=[
            pltpu.VMEM((2, NX * both, 512), F32),
            pltpu.VMEM((2, NX * both, 128), F32),
        ],
    )(
        decay_rate, decay_other, *pieces, attend_own, value_own, rate_own, attend_other,
        value_other, rate_other,
    )

    mix, arrived, shares = lax.optimization_barrier((mix, arrived, shares))
    from_other = swap(arrived)
    *partial, keep, give = pl.pallas_call(
        state_kernel,
        in_specs=[smem] * 2 + [vmem] * 9,
        out_specs=[vmem] * (NX + 2),
        out_shape=[jax.ShapeDtypeStruct((both, model), BF16)] * NX
        + [
            jax.ShapeDtypeStruct((NX, 2, 128, 128), F32),
            jax.ShapeDtypeStruct((NX, 2, 128, 128), F32),
        ],
        scratch_shapes=[pltpu.VMEM((NX * both, 512), BF16)],
    )(resume_from, spot, gates, mix, base, keys, close, arrived, from_other, out_own, out_other)
    final_state = in_order(keep, swap(give))

    def gather_sum(values):
        parts = [lax.ppermute(values[dx], "exp", collect(dx)) for dx in range(NX)]
        total = parts[0].astype(F32)
        for part in parts[1:]:
            total = total + part.astype(F32)
        return total

    attended = gather_sum(partial)
    attended = attended + swap(attended.astype(BF16)).astype(F32)
    hidden = token_rows.astype(F32) + attended
    hidden_normed = rms_scale(hidden).astype(BF16)

    seen = spread_all(hidden_normed)
    seen[0], final_state = lax.optimization_barrier((seen[0], final_state))
    hbm = pl.BlockSpec(memory_space=pl.ANY)
    mixture = pl.pallas_call(
        expert_kernel,
        in_specs=[smem] + [vmem] * 5 + [hbm] * 2 + [vmem] * 2,
        out_specs=[vmem] * NX,
        out_shape=[jax.ShapeDtypeStruct((both, model), BF16)] * NX,
        scratch_shapes=[
            pltpu.VMEM(inner_own.shape, BF16),
            pltpu.VMEM(outer_own.shape, BF16),
            pltpu.SemaphoreType.DMA((2,)),
        ],
        compiler_params=pltpu.CompilerParams(vmem_limit_bytes=28 << 20),
    )(
        mine.astype(jnp.int32).reshape(1), *map(on_chip, seen), on_chip(shares), inner_own, outer_own,
        on_chip(inner_other), on_chip(outer_other),
    )
    summed = gather_sum(mixture)
    mine_rows = jnp.where(first, summed[:rows], summed[rows:])
    others_rows = jnp.where(first, summed[rows:], summed[:rows])
    hidden_rows = jnp.where(first, hidden[:rows], hidden[rows:])
    layer_output = hidden_rows + (mine_rows + swap(others_rows.astype(BF16)).astype(F32))
    return (layer_output.astype(BF16), final_state)


def solution(mesh):
    in_specs = (
        P(("rep", "exp"), None),
        P(None, "exp", None),
        P(None, "exp", None),
        P(None, "exp", None),
        P("exp"),
        P("exp", None, None),
        P("rep", "exp", None, None),
        P(),
        P(("rep", "exp"), None),
        P(("rep", "exp"), None),
        P("exp", None, None),
        P("exp", None, None),
    )
    out_specs = (P(("rep", "exp"), None), P("rep", "exp", None, None))

    return jax.shard_map(local, mesh=mesh, in_specs=in_specs, out_specs=out_specs, check_vma=False)
```

profile of v0, /device:TPU:1, one launch (start us, length us, event | category | flops | bytes accessed | tf_op | source)
XLA Modules:
  0.0 145.5 jit_solution(14119269641076118819)
XLA Ops:
  0.6 3.3 %collective-permute-start = (bf16[32,2048]{1,0:T(8,128)(2,1)}, bf16[32,2048]{1,0:T(8,128)(2,1)S(1)}, u32[]{:S(2)}, u32[]{:S(2)}) collective-permute-start(bf16[32,2048]{1,0:T(8,128)(2,1)} %param.12), channel_id=1, source_target_pairs={{0,1},{1,0},{2,3},{3,2},{4,5},{5,4},{6,7},{7,6},{8,9},{9,8},{10,11... | collective-permute-start | bytes 393224 | tf_op jit(solution)/shard_map/ppermute | solution.py:287
  3.9 2.8 %shard_map.131 = bf16[16,2,128,128]{3,2,1,0:T(8,128)(2,1)} custom-call(s32[128]{0:T(128)} %resume_ref.3, f32[8,2,128,128]{3,2,1,0:T(8,128)} %cache_ref.1), custom_call_target="tpu_custom_call" | custom-call | tf_op jit(solution)/shard_map/pallas_call | solution.py:300
  6.8 1.9 %copy.20 = bf16[2048,2,256]{2,0,1:T(8,128)(2,1)S(1)} copy(bf16[2048,2,256]{2,1,0:T(2,128)(2,1)} %param.14) | data formatting | bytes 4194304 | tf_op jit(solution)/shard_map/optimization_barrier | solution.py:323
  8.7 0.1 collective-permute-start.13
  8.8 9.3 %all-to-all-start = ((bf16[16,2,128,128]{3,2,1,0:T(8,128)(2,1)}), bf16[16,2,128,128]{3,2,1,0:T(8,128)(2,1)S(1)}, u32[]{:S(2)}, u32[]{:S(2)}) async-start(bf16[16,2,128,128]{3,2,1,0:T(8,128)(2,1)} %shard_map.131), calls=%async_computation | async-start | bytes 2097152 | tf_op jit(solution)/shard_map/all_to_all | solution.py:312
  18.2 2.8 %collective-permute-start.1 = (bf16[64,2048]{1,0:T(8,128)(2,1)S(1)}, bf16[64,2048]{1,0:T(8,128)(2,1)}, u32[]{:S(2)}, u32[]{:S(2)}) collective-permute-start(bf16[64,2048]{1,0:T(8,128)(2,1)S(1)} %maximum_select_fusion.1), channel_id=1, source_target_pairs={{0,0},{1,8},{2,2},{3,10},{4,4},{5,12},{6,6},{7,14},{8,9},{9,1},{10... | collective-permute-start | bytes 786440 | tf_op jit(solution)/shard_map/ppermute | solution.py:316
  21.3 0.6 collective-permute-start.10
  21.9 0.1 collective-permute-start.11
  22.0 0.4 collective-permute-done.5
  22.4 0.2 collective-permute-start.12
  22.6 0.5 collective-permute-done.11.decay_other_ref
  23.0 2.8 %collective-permute-start.9 = (f32[64,128]{1,0:T(8,128)S(1)}, f32[64,128]{1,0:T(8,128)S(1)}, u32[]{:S(2)}, u32[]{:S(2)}) collective-permute-start(f32[64,128]{1,0:T(8,128)S(1)} %maximum_select_fusion.2), channel_id=1, source_target_pairs={{0,6},{1,14},{2,0},{3,8},{4,2},{5,10},{6,4},{7,12},{8,15},{9,7},{1... | collective-permute-start | bytes 98312 | tf_op jit(solution)/shard_map/ppermute | solution.py:295
  25.8 0.7 collective-permute-start.8
  26.6 0.7 collective-permute-done.9
  27.3 1.6 %collective-permute-start.7 = (f32[64,128]{1,0:T(8,128)S(1)}, f32[64,128]{1,0:T(8,128)S(1)}, u32[]{:S(2)}, u32[]{:S(2)}) collective-permute-start(f32[64,128]{1,0:T(8,128)S(1)} %maximum_select_fusion.2), channel_id=1, source_target_pairs={{0,2},{1,10},{2,4},{3,12},{4,6},{5,14},{6,0},{7,8},{8,11},{9,3},{1... | collective-permute-start | bytes 98312 | tf_op jit(solution)/shard_map/ppermute | solution.py:295
  28.9 2.5 %collective-permute-done.8 = f32[64,128]{1,0:T(8,128)S(1)} collective-permute-done((f32[64,128]{1,0:T(8,128)S(1)}, f32[64,128]{1,0:T(8,128)S(1)}, u32[]{:S(2)}, u32[]{:S(2)}) %collective-permute-start.8) | collective-permute-done | bytes 32800 | tf_op jit(solution)/shard_map/ppermute | solution.py:295
  31.4 2.6 %collective-permute-start.6 = (f32[64,128]{1,0:T(8,128)S(1)}, f32[64,128]{1,0:T(8,128)S(1)}, u32[]{:S(2)}, u32[]{:S(2)}) collective-permute-start(f32[64,128]{1,0:T(8,128)S(1)} %maximum_select_fusion.2), channel_id=1, source_target_pairs={{0,0},{1,8},{2,2},{3,10},{4,4},{5,12},{6,6},{7,14},{8,9},{9,1},{10... | collective-permute-start | bytes 98312 | tf_op jit(solution)/shard_map/ppermute | solution.py:295
  34.1 3.0 %collective-permute-done.6 = f32[64,128]{1,0:T(8,128)S(1)} collective-permute-done((f32[64,128]{1,0:T(8,128)S(1)}, f32[64,128]{1,0:T(8,128)S(1)}, u32[]{:S(2)}, u32[]{:S(2)}) %collective-permute-start.6) | collective-permute-done | bytes 32800 | tf_op jit(solution)/shard_map/ppermute | solution.py:295
  37.1 0.8 collective-permute-start.3
  37.9 1.4 collective-permute-start.4
  39.3 8.1 %collective-permute-done.2.second_ref = bf16[64,2048]{1,0:T(8,128)(2,1)S(1)} collective-permute-done((bf16[64,2048]{1,0:T(8,128)(2,1)S(1)}, bf16[64,2048]{1,0:T(8,128)(2,1)S(1)}, u32[]{:S(2)}, u32[]{:S(2)}) %collective-permute-start.2) | collective-permute-done | bytes 262176 | tf_op jit(solution)/shard_map/ppermute | solution.py:316
  47.4 4.5 %collective-permute-done.3.third_ref = bf16[64,2048]{1,0:T(8,128)(2,1)S(1)} collective-permute-done((bf16[64,2048]{1,0:T(8,128)(2,1)S(1)}, bf16[64,2048]{1,0:T(8,128)(2,1)S(1)}, u32[]{:S(2)}, u32[]{:S(2)}) %collective-permute-start.3) | collective-permute-done | bytes 262176 | tf_op jit(solution)/shard_map/ppermute | solution.py:316
  51.9 0.7 copy-done.7
  52.7 0.5 collective-permute-start.15
  53.2 12.6 %shard_map.132 = (f32[4,4,128,128]{3,2,1,0:T(8,128)}, f32[4,4,128,128]{3,2,1,0:T(8,128)}, f32[4,4,64,128]{3,2,1,0:T(8,128)}, f32[4,4,1,128]{3,2,1,0:T(1,128)}, f32[256,512]{1,0:T(8,128)}) custom-call(f32[2]{0:T(128)} %decay_own_ref.1, f32[2]{0:T(128)} %copy-done.16, bf16[64,2048]{1,0:T(8,128)(2,1)} %collective-permute-done.1.first_ref, ...), custom_call_target="tpu_custom_call" | custom-call | tf_op jit(solution)/shard_map/pallas_call | solution.py:348
  65.8 0.1 collective-permute-start.14
  65.9 0.8 pad_add_fusion.spot_ref
  66.7 1.8 %collective-permute-done.14.sent_ref = bf16[16,2,128,128]{3,2,1,0:T(8,128)(2,1)S(1)} collective-permute-done((bf16[16,2,128,128]{3,2,1,0:T(8,128)(2,1)S(1)}, bf16[16,2,128,128]{3,2,1,0:T(8,128)(2,1)S(1)}, u32[]{:S(2)}, u32[]{:S(2)}) %collective-permute-start.14) | collective-permute-done | bytes 1048608 | tf_op jit(solution)/shard_map/ppermute | solution.py:287
  68.5 1.0 copy-done.4
  69.5 6.1 %shard_map.133 = (bf16[64,2048]{1,0:T(8,128)(2,1)}, bf16[64,2048]{1,0:T(8,128)(2,1)}, bf16[64,2048]{1,0:T(8,128)(2,1)}, bf16[64,2048]{1,0:T(8,128)(2,1)}, f32[4,...) custom-call(s32[128]{0:T(128)} %resume_ref.3, s32[3]{0:T(128)} %pad_add_fusion.spot_ref, ...), custom_call_target="tpu_custom_call" | custom-call | tf_op jit(solution)/shard_map/pallas_call | solution.py:370
  75.7 2.0 %collective-permute-start.19 = (bf16[64,2048]{1,0:T(8,128)(2,1)}, bf16[64,2048]{1,0:T(8,128)(2,1)S(1)}, u32[]{:S(2)}, u32[]{:S(2)}) collective-permute-start(bf16[64,2048]{1,0:T(8,128)(2,1)} %get-tuple-element.58), channel_id=1, source_target_pairs={{6,0},{14,1},{0,2},{8,3},{2,4},{10,5},{4,6},{12,7},{15,8},{7,9},{9... | collective-permute-start | bytes 786440 | tf_op jit(solution)/shard_map/ppermute | solution.py:384
  77.6 2.6 %collective-permute-start.18 = (bf16[64,2048]{1,0:T(8,128)(2,1)}, bf16[64,2048]{1,0:T(8,128)(2,1)S(1)}, u32[]{:S(2)}, u32[]{:S(2)}) collective-permute-start(bf16[64,2048]{1,0:T(8,128)(2,1)} %get-tuple-element.57), channel_id=1, source_target_pairs={{4,0},{12,1},{6,2},{14,3},{0,4},{8,5},{2,6},{10,7},{13,8},{5,9},{1... | collective-permute-start | bytes 786440 | tf_op jit(solution)/shard_map/ppermute | solution.py:384
  80.2 4.2 %collective-permute-start.17 = (bf16[64,2048]{1,0:T(8,128)(2,1)}, bf16[64,2048]{1,0:T(8,128)(2,1)S(1)}, u32[]{:S(2)}, u32[]{:S(2)}) collective-permute-start(bf16[64,2048]{1,0:T(8,128)(2,1)} %get-tuple-element.56), channel_id=1, source_target_pairs={{2,0},{10,1},{4,2},{12,3},{6,4},{14,5},{0,6},{8,7},{11,8},{3,9},{1... | collective-permute-start | bytes 786440 | tf_op jit(solution)/shard_map/ppermute | solution.py:384
  84.4 2.0 %collective-permute-start.16 = (bf16[64,2048]{1,0:T(8,128)(2,1)}, bf16[64,2048]{1,0:T(8,128)(2,1)S(1)}, u32[]{:S(2)}, u32[]{:S(2)}) collective-permute-start(bf16[64,2048]{1,0:T(8,128)(2,1)} %get-tuple-element.55), channel_id=1, source_target_pairs={{0,0},{8,1},{2,2},{10,3},{4,4},{12,5},{6,6},{14,7},{9,8},{1,9},{11... | collective-permute-start | bytes 786440 | tf_op jit(solution)/shard_map/ppermute | solution.py:384
  86.5 0.2 collective-permute-start.27
  86.6 7.5 %collective-permute-done.18 = bf16[64,2048]{1,0:T(8,128)(2,1)S(1)} collective-permute-done((bf16[64,2048]{1,0:T(8,128)(2,1)}, bf16[64,2048]{1,0:T(8,128)(2,1)S(1)}, u32[]{:S(2)}, u32[]{:S(2)}) %collective-permute-start.18) | collective-permute-done | bytes 262176 | tf_op jit(solution)/shard_map/ppermute | solution.py:384
  94.1 1.4 collective-permute-done.17
  95.5 2.5 %collective-permute-done.16 = bf16[64,2048]{1,0:T(8,128)(2,1)S(1)} collective-permute-done((bf16[64,2048]{1,0:T(8,128)(2,1)}, bf16[64,2048]{1,0:T(8,128)(2,1)S(1)}, u32[]{:S(2)}, u32[]{:S(2)}) %collective-permute-start.16) | collective-permute-done | bytes 262176 | tf_op jit(solution)/shard_map/ppermute | solution.py:384
  98.0 0.1 fusion.2
  98.2 0.3 collective-permute-start.20
  98.5 0.5 collective-permute-start.22
  99.0 1.0 collective-permute-done.20
  100.0 0.3 multiply_reduce_fusion
  100.4 0.1 multiply_convert_fusion
  100.5 1.9 %collective-permute-start.21 = (bf16[64,2048]{1,0:T(8,128)(2,1)S(1)}, bf16[64,2048]{1,0:T(8,128)(2,1)S(1)}, u32[]{:S(2)}, u32[]{:S(2)}) collective-permute-start(bf16[64,2048]{1,0:T(8,128)(2,1)S(1)} %multiply_convert_fusion), channel_id=1, source_target_pairs={{0,0},{1,8},{2,2},{3,10},{4,4},{5,12},{6,6},{7,14},{8,9},{9,1},{10... | collective-permute-start | bytes 786440 | tf_op jit(solution)/shard_map/ppermute | solution.py:295
  102.4 0.1 collective-permute-start.23
  102.5 1.5 %collective-permute-start.24 = (bf16[64,2048]{1,0:T(8,128)(2,1)S(1)}, bf16[64,2048]{1,0:T(8,128)(2,1)S(1)}, u32[]{:S(2)}, u32[]{:S(2)}) collective-permute-start(bf16[64,2048]{1,0:T(8,128)(2,1)S(1)} %multiply_convert_fusion), channel_id=1, source_target_pairs={{0,4},{1,12},{2,6},{3,14},{4,0},{5,8},{6,2},{7,10},{8,13},{9,5},{1... | collective-permute-start | bytes 786440 | tf_op jit(solution)/shard_map/ppermute | solution.py:295
  104.0 5.3 %collective-permute-done.21.first_ref = bf16[64,2048]{1,0:T(8,128)(2,1)S(1)} collective-permute-done((bf16[64,2048]{1,0:T(8,128)(2,1)S(1)}, bf16[64,2048]{1,0:T(8,128)(2,1)S(1)}, u32[]{:S(2)}, u32[]{:S(2)}) %collective-permute-start.21) | collective-permute-done | bytes 262176 | tf_op jit(solution)/shard_map/ppermute | solution.py:295
  109.3 1.1 maximum_select_fusion
  110.4 7.0 %collective-permute-done.23.second_ref = bf16[64,2048]{1,0:T(8,128)(2,1)S(1)} collective-permute-done((bf16[64,2048]{1,0:T(8,128)(2,1)S(1)}, bf16[64,2048]{1,0:T(8,128)(2,1)S(1)}, u32[]{:S(2)}, u32[]{:S(2)}) %collective-permute-start.23) | collective-permute-done | bytes 262176 | tf_op jit(solution)/shard_map/ppermute | solution.py:295
  117.4 0.8 collective-permute-done.25.fourth_ref
  118.2 6.5 %shard_map.134 = (bf16[64,2048]{1,0:T(8,128)(2,1)S(1)}, bf16[64,2048]{1,0:T(8,128)(2,1)S(1)}, bf16[64,2048]{1,0:T(8,128)(2,1)S(1)}, bf16[64,2048]{1,0:T(8,128)(2,1)S(1)}) custom-call(s32[1]{0:T(128)} %bitcast.9.mine_ref, bf16[64,2048]{1,0:T(8,128)(2,1)S(1)} %collective-permute-done.21.first_ref, bf16[64,2048]{1,0:T(8,128)(2,1)S(1)} %collective-permute-done.23.second_ref, ...), custom_call_target="tpu_custom_call" | custom-call | tf_op jit(solution)/shard_map/pallas_call | solution.py:398
  124.7 0.7 collective-permute-start.31
  125.4 3.6 %collective-permute-start.30 = (bf16[64,2048]{1,0:T(8,128)(2,1)S(1)}, bf16[64,2048]{1,0:T(8,128)(2,1)S(1)}, u32[]{:S(2)}, u32[]{:S(2)}) collective-permute-start(bf16[64,2048]{1,0:T(8,128)(2,1)S(1)} %get-tuple-element.67), channel_id=1, source_target_pairs={{4,0},{12,1},{6,2},{14,3},{0,4},{8,5},{2,6},{10,7},{13,8},{5,9},{1... | collective-permute-start | bytes 786440 | tf_op jit(solution)/shard_map/ppermute | solution.py:384
  129.0 0.2 collective-permute-start.29
  129.2 2.9 %collective-permute-start.28 = (bf16[64,2048]{1,0:T(8,128)(2,1)S(1)}, bf16[64,2048]{1,0:T(8,128)(2,1)S(1)}, u32[]{:S(2)}, u32[]{:S(2)}) collective-permute-start(bf16[64,2048]{1,0:T(8,128)(2,1)S(1)} %get-tuple-element.65), channel_id=1, source_target_pairs={{0,0},{8,1},{2,2},{10,3},{4,4},{12,5},{6,6},{14,7},{9,8},{1,9},{11... | collective-permute-start | bytes 786440 | tf_op jit(solution)/shard_map/ppermute | solution.py:384
  132.1 4.4 %collective-permute-done.31 = bf16[64,2048]{1,0:T(8,128)(2,1)S(1)} collective-permute-done((bf16[64,2048]{1,0:T(8,128)(2,1)S(1)}, bf16[64,2048]{1,0:T(8,128)(2,1)S(1)}, u32[]{:S(2)}, u32[]{:S(2)}) %collective-permute-start.31) | collective-permute-done | bytes 262176 | tf_op jit(solution)/shard_map/ppermute | solution.py:384
  136.6 5.7 %collective-permute-done.30 = bf16[64,2048]{1,0:T(8,128)(2,1)S(1)} collective-permute-done((bf16[64,2048]{1,0:T(8,128)(2,1)S(1)}, bf16[64,2048]{1,0:T(8,128)(2,1)S(1)}, u32[]{:S(2)}, u32[]{:S(2)}) %collective-permute-start.30) | collective-permute-done | bytes 262176 | tf_op jit(solution)/shard_map/ppermute | solution.py:384
  142.3 0.3 collective-permute-done.29
  142.6 0.5 collective-permute-done.28
  143.1 0.1 convert_add_fusion
  143.3 0.1 collective-permute-start.32
  143.4 1.3 collective-permute-done.32
  144.7 0.7 fusion.1
  (60 shorter events, 0.6 us)
Async XLA Ops:
  0.6 6.1 %copy-start.10 = (bf16[32,2048]{1,0:T(8,128)(2,1)S(1)}, bf16[32,2048]{1,0:T(8,128)(2,1)}, u32[]{:S(2)}) copy-start(bf16[32,2048]{1,0:T(8,128)(2,1)} %param.12) | copy-start | bytes 393220
  0.6 6.1 %collective-permute-start = (bf16[32,2048]{1,0:T(8,128)(2,1)}, bf16[32,2048]{1,0:T(8,128)(2,1)S(1)}, u32[]{:S(2)}, u32[]{:S(2)}) collective-permute-start(bf16[32,2048]{1,0:T(8,128)(2,1)} %param.12), channel_id=1, source_target_pairs={{0,1},{1,0},{2,3},{3,2},{4,5},{5,4},{6,7},{7,6},{8,9},{9,8},{10,11... | collective-permute-start | bytes 393224 | tf_op jit(solution)/shard_map/ppermute | solution.py:287
  8.7 44.5 %copy-start.2 = (bf16[2048,2,256]{2,0,1:T(8,128)(2,1)}, bf16[2048,2,256]{2,0,1:T(8,128)(2,1)S(1)}, u32[]{:S(2)}) copy-start(bf16[2048,2,256]{2,0,1:T(8,128)(2,1)S(1)} %copy.20) | copy-start | bytes 6291460
  8.7 12.3 %copy-start.13 = (f32[32,10]{0,1:T(8,128)S(1)}, f32[32,10]{0,1:T(8,128)}, u32[]{:S(2)}) copy-start(f32[32,10]{0,1:T(8,128)} %param.21) | copy-start | bytes 3844
  8.7 12.3 %copy-start.14 = (s32[32,10]{0,1:T(8,128)S(1)}, s32[32,10]{0,1:T(8,128)}, u32[]{:S(2)}) copy-start(s32[32,10]{0,1:T(8,128)} %param.20) | copy-start | bytes 3844
  8.7 12.5 %copy-start.12 = (bf16[2048,2,2]{0,2,1:T(2,128)(2,1)S(1)}, bf16[2048,2,2]{0,2,1:T(2,128)(2,1)}, u32[]{:S(2)}) copy-start(bf16[2048,2,2]{0,2,1:T(2,128)(2,1)} %param.15) | copy-start | bytes 49156
  8.7 13.2 %copy-start.15 = (f32[2]{0:T(128)S(1)}, f32[2]{0:T(128)}, u32[]{:S(2)}) copy-start(f32[2]{0:T(128)} %decay_own_ref.1) | copy-start | bytes 28
  8.7 44.5 %collective-permute-start.13 = (bf16[2,2048,256]{2,1,0:T(8,128)(2,1)S(1)}, bf16[2,2048,256]{2,1,0:T(8,128)(2,1)}, u32[]{:S(2)}, u32[]{:S(2)}) collective-permute-start(bf16[2,2048,256]{2,1,0:T(8,128)(2,1)S(1)} %bitcast.16), channel_id=1, source_target_pairs={{0,1},{1,0},{2,3},{3,2},{4,5},{5,4},{6,7},{7,6},{8,9},{9,8},{10,11... | collective-permute-start | bytes 6291464 | tf_op jit(solution)/shard_map/ppermute | solution.py:287
  8.8 56.9 %all-to-all-start = ((bf16[16,2,128,128]{3,2,1,0:T(8,128)(2,1)}), bf16[16,2,128,128]{3,2,1,0:T(8,128)(2,1)S(1)}, u32[]{:S(2)}, u32[]{:S(2)}) async-start(bf16[16,2,128,128]{3,2,1,0:T(8,128)(2,1)} %shard_map.131), calls=%async_computation | async-start | bytes 2097152 | tf_op jit(solution)/shard_map/all_to_all | solution.py:312
  18.2 19.7 %collective-permute-start.1 = (bf16[64,2048]{1,0:T(8,128)(2,1)S(1)}, bf16[64,2048]{1,0:T(8,128)(2,1)}, u32[]{:S(2)}, u32[]{:S(2)}) collective-permute-start(bf16[64,2048]{1,0:T(8,128)(2,1)S(1)} %maximum_select_fusion.1), channel_id=1, source_target_pairs={{0,0},{1,8},{2,2},{3,10},{4,4},{5,12},{6,6},{7,14},{8,9},{9,1},{10... | collective-permute-start | bytes 786440 | tf_op jit(solution)/shard_map/ppermute | solution.py:316
  21.1 1.2 collective-permute-start.5
  21.3 12.7 %copy-start.9 = (bf16[8,2048]{1,0:T(8,128)(2,1)}, bf16[8,2048]{1,0:T(8,128)(2,1)S(1)}, u32[]{:S(2)}) copy-start(bf16[8,2048]{1,0:T(8,128)(2,1)S(1)} %pad.9.rate_own_ref) | copy-start | bytes 98308
  21.3 4.5 %collective-permute-start.10 = (bf16[8,2048]{1,0:T(8,128)(2,1)S(1)}, bf16[8,2048]{1,0:T(8,128)(2,1)S(1)}, u32[]{:S(2)}, u32[]{:S(2)}) collective-permute-start(bf16[8,2048]{1,0:T(8,128)(2,1)S(1)} %pad.9.rate_own_ref), channel_id=1, source_target_pairs={{0,1},{1,0},{2,3},{3,2},{4,5},{5,4},{6,7},{7,6},{8,9},{9,8},{10,11... | collective-permute-start | bytes 98312 | tf_op jit(solution)/shard_map/ppermute | solution.py:287
  21.9 1.2 collective-permute-start.11
  22.4 30.8 %collective-permute-start.12 = (bf16[2048,256]{1,0:T(8,128)(2,1)}, bf16[2048,256]{1,0:T(8,128)(2,1)}, u32[]{:S(2)}, u32[]{:S(2)}) collective-permute-start(bf16[2048,256]{1,0:T(8,128)(2,1)} %bitcast.20), channel_id=1, source_target_pairs={{0,1},{1,0},{2,3},{3,2},{4,5},{5,4},{6,7},{7,6},{8,9},{9,8},{10,11... | collective-permute-start | bytes 3145736 | tf_op jit(solution)/shard_map/ppermute | solution.py:287
  23.0 30.2 %copy-start.16 = (f32[2]{0:T(128)}, f32[2]{0:T(128)S(1)}, u32[]{:S(2)}) copy-start(f32[2]{0:T(128)S(1)} %collective-permute-done.11.decay_other_ref) | copy-start | bytes 28
  23.0 4.3 %collective-permute-start.9 = (f32[64,128]{1,0:T(8,128)S(1)}, f32[64,128]{1,0:T(8,128)S(1)}, u32[]{:S(2)}, u32[]{:S(2)}) collective-permute-start(f32[64,128]{1,0:T(8,128)S(1)} %maximum_select_fusion.2), channel_id=1, source_target_pairs={{0,6},{1,14},{2,0},{3,8},{4,2},{5,10},{6,4},{7,12},{8,15},{9,7},{1... | collective-permute-start | bytes 98312 | tf_op jit(solution)/shard_map/ppermute | solution.py:295
  25.8 12.1 %copy-start.11 = (bf16[8,2048]{1,0:T(8,128)(2,1)}, bf16[8,2048]{1,0:T(8,128)(2,1)S(1)}, u32[]{:S(2)}) copy-start(bf16[8,2048]{1,0:T(8,128)(2,1)S(1)} %collective-permute-done.10.rate_other_ref) | copy-start | bytes 98308
  25.8 5.6 %collective-permute-start.8 = (f32[64,128]{1,0:T(8,128)S(1)}, f32[64,128]{1,0:T(8,128)S(1)}, u32[]{:S(2)}, u32[]{:S(2)}) collective-permute-start(f32[64,128]{1,0:T(8,128)S(1)} %maximum_select_fusion.2), channel_id=1, source_target_pairs={{0,4},{1,12},{2,6},{3,14},{4,0},{5,8},{6,2},{7,10},{8,13},{9,5},{1... | collective-permute-start | bytes 98312 | tf_op jit(solution)/shard_map/ppermute | solution.py:295
  27.3 6.7 %collective-permute-start.7 = (f32[64,128]{1,0:T(8,128)S(1)}, f32[64,128]{1,0:T(8,128)S(1)}, u32[]{:S(2)}, u32[]{:S(2)}) collective-permute-start(f32[64,128]{1,0:T(8,128)S(1)} %maximum_select_fusion.2), channel_id=1, source_target_pairs={{0,2},{1,10},{2,4},{3,12},{4,6},{5,14},{6,0},{7,8},{8,11},{9,3},{1... | collective-permute-start | bytes 98312 | tf_op jit(solution)/shard_map/ppermute | solution.py:295
  31.4 5.7 %collective-permute-start.6 = (f32[64,128]{1,0:T(8,128)S(1)}, f32[64,128]{1,0:T(8,128)S(1)}, u32[]{:S(2)}, u32[]{:S(2)}) collective-permute-start(f32[64,128]{1,0:T(8,128)S(1)} %maximum_select_fusion.2), channel_id=1, source_target_pairs={{0,0},{1,8},{2,2},{3,10},{4,4},{5,12},{6,6},{7,14},{8,9},{9,1},{10... | collective-permute-start | bytes 98312 | tf_op jit(solution)/shard_map/ppermute | solution.py:295
  34.0 13.3 %collective-permute-start.2 = (bf16[64,2048]{1,0:T(8,128)(2,1)S(1)}, bf16[64,2048]{1,0:T(8,128)(2,1)S(1)}, u32[]{:S(2)}, u32[]{:S(2)}) collective-permute-start(bf16[64,2048]{1,0:T(8,128)(2,1)S(1)} %maximum_select_fusion.1), channel_id=1, source_target_pairs={{0,2},{1,10},{2,4},{3,12},{4,6},{5,14},{6,0},{7,8},{8,11},{9,3},{1... | collective-permute-start | bytes 786440 | tf_op jit(solution)/shard_map/ppermute | solution.py:316
  37.1 14.7 %collective-permute-start.3 = (bf16[64,2048]{1,0:T(8,128)(2,1)S(1)}, bf16[64,2048]{1,0:T(8,128)(2,1)S(1)}, u32[]{:S(2)}, u32[]{:S(2)}) collective-permute-start(bf16[64,2048]{1,0:T(8,128)(2,1)S(1)} %maximum_select_fusion.1), channel_id=1, source_target_pairs={{0,4},{1,12},{2,6},{3,14},{4,0},{5,8},{6,2},{7,10},{8,13},{9,5},{1... | collective-permute-start | bytes 786440 | tf_op jit(solution)/shard_map/ppermute | solution.py:316
  37.9 14.0 %collective-permute-start.4 = (bf16[64,2048]{1,0:T(8,128)(2,1)S(1)}, bf16[64,2048]{1,0:T(8,128)(2,1)S(1)}, u32[]{:S(2)}, u32[]{:S(2)}) collective-permute-start(bf16[64,2048]{1,0:T(8,128)(2,1)S(1)} %maximum_select_fusion.1), channel_id=1, source_target_pairs={{0,6},{1,14},{2,0},{3,8},{4,2},{5,10},{6,4},{7,12},{8,15},{9,7},{1... | collective-permute-start | bytes 786440 | tf_op jit(solution)/shard_map/ppermute | solution.py:316
  47.4 4.5 %copy-start.6 = (bf16[64,2048]{1,0:T(8,128)(2,1)}, bf16[64,2048]{1,0:T(8,128)(2,1)S(1)}, u32[]{:S(2)}) copy-start(bf16[64,2048]{1,0:T(8,128)(2,1)S(1)} %collective-permute-done.2.second_ref) | copy-start | bytes 786436
  51.9 0.7 copy-start.7
  51.9 0.8 copy-start.8
  52.7 65.6 %collective-permute-start.26 = (bf16[2048,1024]{1,0:T(8,128)(2,1)}, bf16[2048,1024]{1,0:T(8,128)(2,1)}, u32[]{:S(2)}, u32[]{:S(2)}) collective-permute-start(bf16[2048,1024]{1,0:T(8,128)(2,1)} %bitcast.12), channel_id=1, source_target_pairs={{0,1},{1,0},{2,3},{3,2},{4,5},{5,4},{6,7},{7,6},{8,9},{9,8},{10,11... | collective-permute-start | bytes 12582920 | tf_op jit(solution)/shard_map/ppermute | solution.py:287
  52.7 14.0 %collective-permute-start.15 = (bf16[256,2048]{1,0:T(8,128)(2,1)}, bf16[256,2048]{1,0:T(8,128)(2,1)}, u32[]{:S(2)}, u32[]{:S(2)}) collective-permute-start(bf16[256,2048]{1,0:T(8,128)(2,1)} %bitcast.18), channel_id=1, source_target_pairs={{0,1},{1,0},{2,3},{3,2},{4,5},{5,4},{6,7},{7,6},{8,9},{9,8},{10,11... | collective-permute-start | bytes 3145736 | tf_op jit(solution)/shard_map/ppermute | solution.py:287
  65.8 3.8 %copy-start.3 = (bf16[16,2,128,128]{3,2,1,0:T(8,128)(2,1)}, bf16[16,2,128,128]{3,2,1,0:T(8,128)(2,1)S(1)}, u32[]{:S(2)}) copy-start(bf16[16,2,128,128]{3,2,1,0:T(8,128)(2,1)S(1)} %all-to-all-done.held_ref) | copy-start | bytes 3145732
  65.8 2.7 %collective-permute-start.14 = (bf16[16,2,128,128]{3,2,1,0:T(8,128)(2,1)S(1)}, bf16[16,2,128,128]{3,2,1,0:T(8,128)(2,1)S(1)}, u32[]{:S(2)}, u32[]{:S(2)}) collective-permute-start(bf16[16,2,128,128]{3,2,1,0:T(8,128)(2,1)S(1)} %all-to-all-done.held_ref), channel_id=1, source_target_pairs={{0,1},{1,0},{2,3},{3,2},{4,5},{5,4},{6,7},{7,6},{8,9},{9,8},{10,11... | collective-permute-start | bytes 3145736 | tf_op jit(solution)/shard_map/ppermute | solution.py:287
  68.5 1.0 copy-start.4
  69.5 16.9 %copy-start.1 = (bf16[1,512,2048]{2,1,0:T(8,128)(2,1)S(1)}, bf16[1,512,2048]{2,1,0:T(8,128)(2,1)}, u32[]{:S(2)}) copy-start(bf16[1,512,2048]{2,1,0:T(8,128)(2,1)} %param.23) | copy-start | bytes 6291460
  75.7 10.8 %collective-permute-start.19 = (bf16[64,2048]{1,0:T(8,128)(2,1)}, bf16[64,2048]{1,0:T(8,128)(2,1)S(1)}, u32[]{:S(2)}, u32[]{:S(2)}) collective-permute-start(bf16[64,2048]{1,0:T(8,128)(2,1)} %get-tuple-element.58), channel_id=1, source_target_pairs={{6,0},{14,1},{0,2},{8,3},{2,4},{10,5},{4,6},{12,7},{15,8},{7,9},{9... | collective-permute-start | bytes 786440 | tf_op jit(solution)/shard_map/ppermute | solution.py:384
  77.6 16.5 %collective-permute-start.18 = (bf16[64,2048]{1,0:T(8,128)(2,1)}, bf16[64,2048]{1,0:T(8,128)(2,1)S(1)}, u32[]{:S(2)}, u32[]{:S(2)}) collective-permute-start(bf16[64,2048]{1,0:T(8,128)(2,1)} %get-tuple-element.57), channel_id=1, source_target_pairs={{4,0},{12,1},{6,2},{14,3},{0,4},{8,5},{2,6},{10,7},{13,8},{5,9},{1... | collective-permute-start | bytes 786440 | tf_op jit(solution)/shard_map/ppermute | solution.py:384
  80.2 15.3 %collective-permute-start.17 = (bf16[64,2048]{1,0:T(8,128)(2,1)}, bf16[64,2048]{1,0:T(8,128)(2,1)S(1)}, u32[]{:S(2)}, u32[]{:S(2)}) collective-permute-start(bf16[64,2048]{1,0:T(8,128)(2,1)} %get-tuple-element.56), channel_id=1, source_target_pairs={{2,0},{10,1},{4,2},{12,3},{6,4},{14,5},{0,6},{8,7},{11,8},{3,9},{1... | collective-permute-start | bytes 786440 | tf_op jit(solution)/shard_map/ppermute | solution.py:384
  84.4 24.9 %copy-start.5 = (f32[4,2,128,128]{3,2,1,0:T(8,128)S(1)}, f32[4,2,128,128]{3,2,1,0:T(8,128)}, u32[]{:S(2)}) copy-start(f32[4,2,128,128]{3,2,1,0:T(8,128)} %get-tuple-element.59) | copy-start | bytes 1572868
  84.4 13.6 %collective-permute-start.16 = (bf16[64,2048]{1,0:T(8,128)(2,1)}, bf16[64,2048]{1,0:T(8,128)(2,1)S(1)}, u32[]{:S(2)}, u32[]{:S(2)}) collective-permute-start(bf16[64,2048]{1,0:T(8,128)(2,1)} %get-tuple-element.55), channel_id=1, source_target_pairs={{0,0},{8,1},{2,2},{10,3},{4,4},{12,5},{6,6},{14,7},{9,8},{1,9},{11... | collective-permute-start | bytes 786440 | tf_op jit(solution)/shard_map/ppermute | solution.py:384
  86.5 23.9 %collective-permute-start.27 = (bf16[512,2048]{1,0:T(8,128)(2,1)S(1)}, bf16[512,2048]{1,0:T(8,128)(2,1)S(1)}, u32[]{:S(2)}, u32[]{:S(2)}) collective-permute-start(bf16[512,2048]{1,0:T(8,128)(2,1)S(1)} %bitcast.14), channel_id=1, source_target_pairs={{0,1},{1,0},{2,3},{3,2},{4,5},{5,4},{6,7},{7,6},{8,9},{9,8},{10,11... | collective-permute-start | bytes 6291464 | tf_op jit(solution)/shard_map/ppermute | solution.py:287
  98.2 1.8 %collective-permute-start.20 = (bf16[64,2048]{1,0:T(8,128)(2,1)S(1)}, bf16[64,2048]{1,0:T(8,128)(2,1)S(1)}, u32[]{:S(2)}, u32[]{:S(2)}) collective-permute-start(bf16[64,2048]{1,0:T(8,128)(2,1)S(1)} %fusion.2), channel_id=1, source_target_pairs={{0,1},{1,0},{2,3},{3,2},{4,5},{5,4},{6,7},{7,6},{8,9},{9,8},{10,11... | collective-permute-start | bytes 786440 | tf_op jit(solution)/shard_map/ppermute | solution.py:287
  98.5 19.8 %copy-start = (bf16[1,2048,1024]{2,1,0:T(8,128)(2,1)S(1)}, bf16[1,2048,1024]{2,1,0:T(8,128)(2,1)}, u32[]{:S(2)}) copy-start(bf16[1,2048,1024]{2,1,0:T(8,128)(2,1)} %param.22) | copy-start | bytes 12582916
  98.5 4.0 %collective-permute-start.22 = (f32[4,2,128,128]{3,2,1,0:T(8,128)}, f32[4,2,128,128]{3,2,1,0:T(8,128)S(1)}, u32[]{:S(2)}, u32[]{:S(2)}) collective-permute-start(f32[4,2,128,128]{3,2,1,0:T(8,128)} %get-tuple-element.60), channel_id=1, source_target_pairs={{0,1},{1,0},{2,3},{3,2},{4,5},{5,4},{6,7},{7,6},{8,9},{9,8},{10,11... | collective-permute-start | bytes 1572872 | tf_op jit(solution)/shard_map/ppermute | solution.py:287
  100.5 8.8 %collective-permute-start.21 = (bf16[64,2048]{1,0:T(8,128)(2,1)S(1)}, bf16[64,2048]{1,0:T(8,128)(2,1)S(1)}, u32[]{:S(2)}, u32[]{:S(2)}) collective-permute-start(bf16[64,2048]{1,0:T(8,128)(2,1)S(1)} %multiply_convert_fusion), channel_id=1, source_target_pairs={{0,0},{1,8},{2,2},{3,10},{4,4},{5,12},{6,6},{7,14},{8,9},{9,1},{10... | collective-permute-start | bytes 786440 | tf_op jit(solution)/shard_map/ppermute | solution.py:295
  102.4 15.0 %collective-permute-start.23 = (bf16[64,2048]{1,0:T(8,128)(2,1)S(1)}, bf16[64,2048]{1,0:T(8,128)(2,1)S(1)}, u32[]{:S(2)}, u32[]{:S(2)}) collective-permute-start(bf16[64,2048]{1,0:T(8,128)(2,1)S(1)} %multiply_convert_fusion), channel_id=1, source_target_pairs={{0,2},{1,10},{2,4},{3,12},{4,6},{5,14},{6,0},{7,8},{8,11},{9,3},{1... | collective-permute-start | bytes 786440 | tf_op jit(solution)/shard_map/ppermute | solution.py:295
  102.5 14.9 %collective-permute-start.24 = (bf16[64,2048]{1,0:T(8,128)(2,1)S(1)}, bf16[64,2048]{1,0:T(8,128)(2,1)S(1)}, u32[]{:S(2)}, u32[]{:S(2)}) collective-permute-start(bf16[64,2048]{1,0:T(8,128)(2,1)S(1)} %multiply_convert_fusion), channel_id=1, source_target_pairs={{0,4},{1,12},{2,6},{3,14},{4,0},{5,8},{6,2},{7,10},{8,13},{9,5},{1... | collective-permute-start | bytes 786440 | tf_op jit(solution)/shard_map/ppermute | solution.py:295
  109.3 8.9 %collective-permute-start.25 = (bf16[64,2048]{1,0:T(8,128)(2,1)S(1)}, bf16[64,2048]{1,0:T(8,128)(2,1)S(1)}, u32[]{:S(2)}, u32[]{:S(2)}) collective-permute-start(bf16[64,2048]{1,0:T(8,128)(2,1)S(1)} %multiply_convert_fusion), channel_id=1, source_target_pairs={{0,6},{1,14},{2,0},{3,8},{4,2},{5,10},{6,4},{7,12},{8,15},{9,7},{1... | collective-permute-start | bytes 786440 | tf_op jit(solution)/shard_map/ppermute | solution.py:295
  124.7 11.8 %collective-permute-start.31 = (bf16[64,2048]{1,0:T(8,128)(2,1)S(1)}, bf16[64,2048]{1,0:T(8,128)(2,1)S(1)}, u32[]{:S(2)}, u32[]{:S(2)}) collective-permute-start(bf16[64,2048]{1,0:T(8,128)(2,1)S(1)} %get-tuple-element.68), channel_id=1, source_target_pairs={{6,0},{14,1},{0,2},{8,3},{2,4},{10,5},{4,6},{12,7},{15,8},{7,9},{9... | collective-permute-start | bytes 786440 | tf_op jit(solution)/shard_map/ppermute | solution.py:384
  125.4 16.9 %collective-permute-start.30 = (bf16[64,2048]{1,0:T(8,128)(2,1)S(1)}, bf16[64,2048]{1,0:T(8,128)(2,1)S(1)}, u32[]{:S(2)}, u32[]{:S(2)}) collective-permute-start(bf16[64,2048]{1,0:T(8,128)(2,1)S(1)} %get-tuple-element.67), channel_id=1, source_target_pairs={{4,0},{12,1},{6,2},{14,3},{0,4},{8,5},{2,6},{10,7},{13,8},{5,9},{1... | collective-permute-start | bytes 786440 | tf_op jit(solution)/shard_map/ppermute | solution.py:384
  129.0 13.6 %collective-permute-start.29 = (bf16[64,2048]{1,0:T(8,128)(2,1)S(1)}, bf16[64,2048]{1,0:T(8,128)(2,1)S(1)}, u32[]{:S(2)}, u32[]{:S(2)}) collective-permute-start(bf16[64,2048]{1,0:T(8,128)(2,1)S(1)} %get-tuple-element.66), channel_id=1, source_target_pairs={{2,0},{10,1},{4,2},{12,3},{6,4},{14,5},{0,6},{8,7},{11,8},{3,9},{1... | collective-permute-start | bytes 786440 | tf_op jit(solution)/shard_map/ppermute | solution.py:384
  129.2 13.9 %collective-permute-start.28 = (bf16[64,2048]{1,0:T(8,128)(2,1)S(1)}, bf16[64,2048]{1,0:T(8,128)(2,1)S(1)}, u32[]{:S(2)}, u32[]{:S(2)}) collective-permute-start(bf16[64,2048]{1,0:T(8,128)(2,1)S(1)} %get-tuple-element.65), channel_id=1, source_target_pairs={{0,0},{8,1},{2,2},{10,3},{4,4},{12,5},{6,6},{14,7},{9,8},{1,9},{11... | collective-permute-start | bytes 786440 | tf_op jit(solution)/shard_map/ppermute | solution.py:384
  143.3 1.4 collective-permute-start.32
where the time goes:
time: 146 us; the launch traced here: 145 us
  waiting for transfers between devices  59.4 us (41%)
  starting transfers between devices  49.8 us (34%)
  Pallas kernels  28 us (19%)
  local copies, waits for them, and re-layouts  3.81 us (3%)
  other arithmetic  3.43 us (2%)
    ppermute x8, waiting for transfers between devices, gather_sum(): parts = [lax.ppermute(values[dx], 'exp', collect(dx)) for dx in range(NX)]  22.4 us
    ppermute x8, waiting for transfers between devices, spread_all(): return [lax.ppermute(values, 'exp', spread(dx)) for dx in range(NX)]  19.4 us
    ppermute x8, starting transfers between devices, gather_sum(): parts = [lax.ppermute(values[dx], 'exp', collect(dx)) for dx in range(NX)]  18.2 us
    pallas_call x1, Pallas kernels, local(): pl.pallas_call(chunk_kernel, in_specs=[smem] * 2 + [vmem] * 10, out_specs...  12.6 us
    ppermute x4, waiting for transfers between devices, local(): pieces.append(lax.ppermute(token_rows, 'exp', spread(dx)))  12.6 us
    ppermute x8, starting transfers between devices, spread_all(): return [lax.ppermute(values, 'exp', spread(dx)) for dx in range(NX)]  11.2 us
    all_to_all x1, starting transfers between devices, local(): lax.all_to_all(slots, 'rep', split_axis=0, concat_axis=0, tiled=True)  9.35 us
    pallas_call x1, Pallas kernels, local(): pl.pallas_call(expert_kernel, in_specs=[smem] + [vmem] * 5 + [hbm] * 2 +...  6.48 us
  transfers between devices with their start and end apart: 34, of which 20 were waited for; matrix products, arithmetic and copies ran while one was open for 2% of the time, Pallas kernels for 15%

commit v1 on v0

--- a/solution.py
+++ b/solution.py
@@ -7,6 +7,7 @@
 
 
 EPSILON = 1e-06
+EXPERTS = 16
 F32 = jnp.float32
 BF16 = jnp.bfloat16
 
@@ -35,6 +36,10 @@
 
 def on_chip(values):
     return pltpu.with_memory_space_constraint(values, pltpu.VMEM)
+
+
+def off_chip(values):
+    return pltpu.with_memory_space_constraint(values, pltpu.HBM)
 
 
 def rms_scale(values):
@@ -188,14 +193,16 @@
 
 
 def state_kernel(
-    resume_ref, spot_ref, gate_ref, mix_ref, base_ref, key_ref, close_ref, held_ref, sent_ref, out_own_ref,
+    resume_ref, gate_ref, mix_ref, base_ref, key_ref, close_ref, held_ref, sent_ref, out_own_ref,
     out_other_ref, first_ref, second_ref, third_ref, fourth_ref, keep_ref, give_ref, gated_ref,
 ):
     width = 64
+    mine = lax.axis_index("exp")
+    my_core, my_x = mine % NC, (mine // NC) % NX
     for traj in range(4):
         span = slice(width * traj, width * (traj + 1))
-        to_place = (spot_ref[2] + 4 - traj) % 4
-        from_slot = resume_ref[spot_ref[0] * 8 + spot_ref[1] * 4 + to_place] // 8
+        to_place = (my_x + 4 - traj) % 4
+        from_slot = resume_ref[lax.axis_index("rep") * 8 + my_core * 4 + to_place] // 8
         for part in range(2):
             for head in range(2):
                 unit = part * 2 + head
@@ -225,7 +232,7 @@
 
 
 def expert_kernel(
-    mine_ref, first_ref, second_ref, third_ref, fourth_ref, share_ref, inner_own_ref, outer_own_ref,
+    mine_ref, first_ref, second_ref, third_ref, fourth_ref, inner_own_ref, outer_own_ref,
     inner_other_ref, outer_other_ref, *rest,
 ):
     *out_refs, inner_ref, outer_ref, sems = rest
@@ -235,10 +242,11 @@
     ]
     for fetch in fetches:
         fetch.start()
-    rows = jnp.concatenate(
-        [first_ref[...], second_ref[...], third_ref[...], fourth_ref[...]], axis=0
-    )
-    column = lax.broadcasted_iota(jnp.int32, share_ref.shape, 1)
+    model = inner_ref.shape[0]
+    refs = (first_ref, second_ref, third_ref, fourth_ref)
+    rows = jnp.concatenate([ref[:, :model] for ref in refs], axis=0)
+    share = jnp.concatenate([ref[:, model:] for ref in refs], axis=0).astype(F32)
+    column = lax.broadcasted_iota(jnp.int32, share.shape, 1) % EXPERTS
     total = None
     for number, inner, outer in (
         (mine_ref[0] ^ 1, inner_other_ref, outer_other_ref),
@@ -253,7 +261,7 @@
         if total is not None:
             fetches[1].wait()
         produced = dot(activated, outer[...]).astype(BF16).astype(F32)
-        weight = jnp.sum(jnp.where(column == number, share_ref[...], 0.0), axis=1, keepdims=True)
+        weight = jnp.sum(jnp.where(column == number, share, 0.0), axis=1, keepdims=True)
         total = weight * produced if total is None else total + weight * produced
     for number, ref in enumerate(out_refs):
         ref[...] = total[64 * number : 64 * (number + 1)].astype(BF16)
@@ -277,10 +285,8 @@
     both = 2 * rows
     trajs = state_cache.shape[0]
     groups = lax.axis_size("rep")
-    me = lax.axis_index("rep")
     mine = lax.axis_index("exp")
     my_core = mine % NC
-    my_x = (mine // NC) % NX
     first = my_core == 0
 
     def swap(values):
@@ -294,7 +300,14 @@
     def spread_all(values):
         return [lax.ppermute(values, "exp", spread(dx)) for dx in range(NX)]
 
-    spot = jnp.stack([me, my_core, my_x]).astype(jnp.int32)
+
+    out_own = output_weight.reshape(-1, model)
+    inner_own, outer_own = expert_inner[0], expert_outer[0]
+    attend_own = attend_weight.reshape(model, -1)
+    attend_other = swap(attend_own)
+    out_other = swap(out_own)
+    inner_other = swap(inner_own)
+    outer_other = swap(outer_own)
 
     heads, dv, dk = state_cache.shape[1:]
     slots = pl.pallas_call(
@@ -315,33 +328,26 @@
     for dx in range(NX):
         pieces.append(lax.ppermute(token_rows, "exp", spread(dx)))
 
-    attend_own = attend_weight.reshape(model, -1)
-    rate_own = jnp.pad(jnp.transpose(rate_weight, (1, 2, 0)).reshape(2 * heads, model), ((0, 4), (0, 0)))
+    rate_own = jnp.transpose(rate_weight, (1, 2, 0)).reshape(2 * heads, model)
+    rate_own = jnp.pad(rate_own, ((0, 8 - 2 * heads), (0, 0)))
     rate_other = swap(rate_own)
     decay_other = swap(decay_rate)
-    attend_other = swap(attend_own)
     token_rows, value_weight = lax.optimization_barrier((token_rows, value_weight))
     value_own = jnp.transpose(value_weight, (1, 0, 2))
     value_other = swap(value_own)
-    out_own = output_weight.reshape(-1, model)
-    inner_own, outer_own = expert_inner[0], expert_outer[0]
-    experts = lax.axis_size("exp")
     share = jnp.sum(
         jnp.where(
-            expert_index[:, :, None] == jnp.arange(experts, dtype=jnp.int32), route_weight[:, :, None], 0.0
+            expert_index[:, :, None] == jnp.arange(EXPERTS, dtype=jnp.int32),
+            route_weight[:, :, None],
+            0.0,
         ),
         axis=1,
     )
-    share = jnp.pad(share, ((0, 0), (0, 128 - experts)))
+    high, rest = halves(share)
+    low = (share - high.astype(F32) - rest.astype(F32)).astype(BF16)
+    share = jnp.concatenate([high, rest, low, jnp.zeros((rows, 128 - 3 * EXPERTS), BF16)], axis=1)
     share_other = swap(share)
-    shares = jnp.concatenate(spread_all(in_order(share, share_other)), axis=0)
-
-    *pieces, shares, rate_other, decay_other, out_sent, inner_sent, outer_sent = (
-        lax.optimization_barrier(
-            (*pieces, shares, rate_other, decay_other, out_own, inner_own, outer_own)
-        )
-    )
-    out_other, inner_other, outer_other = swap(out_sent), swap(inner_sent), swap(outer_sent)
+    share_rows = in_order(share, share_other)
 
     vmem = pl.BlockSpec(memory_space=pltpu.VMEM)
     smem = pl.BlockSpec(memory_space=pltpu.SMEM)
@@ -350,26 +356,27 @@
         in_specs=[smem] * 2 + [vmem] * 10,
         out_specs=[vmem] * 5,
         out_shape=[
-            jax.ShapeDtypeStruct((NX, 4, 128, 128), F32),
-            jax.ShapeDtypeStruct((NX, 4, 128, 128), F32),
-            jax.ShapeDtypeStruct((NX, 4, 64, 128), F32),
-            jax.ShapeDtypeStruct((NX, 4, 1, 128), F32),
-            jax.ShapeDtypeStruct((NX * both, 512), F32),
+            pltpu.HBM((NX, 4, 128, 128), F32),
+            pltpu.HBM((NX, 4, 128, 128), F32),
+            pltpu.HBM((NX, 4, 64, 128), F32),
+            pltpu.HBM((NX, 4, 1, 128), F32),
+            pltpu.HBM((NX * both, 512), F32),
         ],
         scratch_shapes=[
             pltpu.VMEM((2, NX * both, 512), F32),
             pltpu.VMEM((2, NX * both, 128), F32),
         ],
+        compiler_params=pltpu.CompilerParams(vmem_limit_bytes=24 << 20),
     )(
-        decay_rate, decay_other, *pieces, attend_own, value_own, rate_own, attend_other,
-        value_other, rate_other,
-    )
-
-    mix, arrived, shares = lax.optimization_barrier((mix, arrived, shares))
+        decay_rate, decay_other, *pieces, attend_own, on_chip(value_own), rate_own,
+        on_chip(attend_other), on_chip(value_other), rate_other,
+    )
+
+    mix, arrived, share_rows = lax.optimization_barrier((mix, arrived, share_rows))
     from_other = swap(arrived)
     *partial, keep, give = pl.pallas_call(
         state_kernel,
-        in_specs=[smem] * 2 + [vmem] * 9,
+        in_specs=[smem] + [vmem] * 9,
         out_specs=[vmem] * (NX + 2),
         out_shape=[jax.ShapeDtypeStruct((both, model), BF16)] * NX
         + [
@@ -377,7 +384,11 @@
             jax.ShapeDtypeStruct((NX, 2, 128, 128), F32),
         ],
         scratch_shapes=[pltpu.VMEM((NX * both, 512), BF16)],
-    )(resume_from, spot, gates, mix, base, keys, close, arrived, from_other, out_own, out_other)
+        compiler_params=pltpu.CompilerParams(vmem_limit_bytes=20 << 20),
+    )(
+        resume_from, *map(off_chip, (gates, mix, base, keys, close)), on_chip(arrived),
+        on_chip(from_other), off_chip(out_own), off_chip(out_other),
+    )
     final_state = in_order(keep, swap(give))
 
     def gather_sum(values):
@@ -392,12 +403,12 @@
     hidden = token_rows.astype(F32) + attended
     hidden_normed = rms_scale(hidden).astype(BF16)
 
-    seen = spread_all(hidden_normed)
+    hbm = pl.BlockSpec(memory_space=pl.ANY)
+    seen = spread_all(jnp.concatenate([hidden_normed, share_rows], axis=1))
     seen[0], final_state = lax.optimization_barrier((seen[0], final_state))
-    hbm = pl.BlockSpec(memory_space=pl.ANY)
     mixture = pl.pallas_call(
         expert_kernel,
-        in_specs=[smem] + [vmem] * 5 + [hbm] * 2 + [vmem] * 2,
+        in_specs=[smem] + [vmem] * 4 + [hbm] * 2 + [vmem] * 2,
         out_specs=[vmem] * NX,
         out_shape=[jax.ShapeDtypeStruct((both, model), BF16)] * NX,
         scratch_shapes=[
@@ -407,7 +418,7 @@
         ],
         compiler_params=pltpu.CompilerParams(vmem_limit_bytes=28 << 20),
     )(
-        mine.astype(jnp.int32).reshape(1), *map(on_chip, seen), on_chip(shares), inner_own, outer_own,
+        mine.astype(jnp.int32).reshape(1), *map(on_chip, seen), inner_own, outer_own,
         on_chip(inner_other), on_chip(outer_other),
     )
     summed = gather_sum(mixture)

time: 146 us -> 142 us (0.973)
  the two profiles are of different devices: /device:TPU:1 before, /device:TPU:81 now
where the time goes in v1:
time: 142 us; the launch traced here: 141 us
  waiting for transfers between devices  56.7 us (40%)
  starting transfers between devices  51.8 us (36%)
  Pallas kernels  25 us (18%)
  other arithmetic  3.52 us (2%)
  local copies, waits for them, and re-layouts  3.32 us (2%)
    ppermute x8, waiting for transfers between devices, gather_sum(): parts = [lax.ppermute(values[dx], 'exp', collect(dx)) for dx in range(NX)]  27.9 us
    ppermute x8, starting transfers between devices, gather_sum(): parts = [lax.ppermute(values[dx], 'exp', collect(dx)) for dx in range(NX)]  16.7 us
    ppermute x4, starting transfers between devices, local(): pieces.append(lax.ppermute(token_rows, 'exp', spread(dx)))  13.2 us
    ppermute x4, waiting for transfers between devices, local(): pieces.append(lax.ppermute(token_rows, 'exp', spread(dx)))  12 us
    pallas_call x1, Pallas kernels, local(): pl.pallas_call(chunk_kernel, in_specs=[smem] * 2 + [vmem] * 10, out_specs...  11.4 us
    all_to_all x1, starting transfers between devices, local(): lax.all_to_all(slots, 'rep', split_axis=0, concat_axis=0, tiled=True)  9.98 us
    ppermute x4, waiting for transfers between devices, spread_all(): return [lax.ppermute(values, 'exp', spread(dx)) for dx in range(NX)]  9.7 us
    ppermute x4, starting transfers between devices, spread_all(): return [lax.ppermute(values, 'exp', spread(dx)) for dx in range(NX)]  8.35 us
  transfers between devices with their start and end apart: 30, of which 18 were waited for; matrix products, arithmetic and copies ran while one was open for 1% of the time, Pallas kernels for 13%

profile of v1, /device:TPU:81, one launch (start us, length us, event | category | flops | bytes accessed | tf_op | source)
XLA Modules:
  0.0 141.2 jit_solution(8012425234464140529)
XLA Ops:
  0.6 0.8 collective-permute-start
  1.4 2.8 %shard_map.131 = bf16[16,2,128,128]{3,2,1,0:T(8,128)(2,1)} custom-call(s32[128]{0:T(128)} %resume_ref.3, f32[8,2,128,128]{3,2,1,0:T(8,128)} %cache_ref.1), custom_call_target="tpu_custom_call" | custom-call | tf_op jit(solution)/shard_map/pallas_call | solution.py:313
  4.2 0.7 maximum_select_fusion.1
  4.9 1.9 %copy.25 = bf16[2048,2,256]{2,0,1:T(8,128)(2,1)S(1)} copy(bf16[2048,2,256]{2,1,0:T(2,128)(2,1)} %param.14) | data formatting | bytes 4194304 | tf_op jit(solution)/shard_map/optimization_barrier | solution.py:335
  6.9 0.1 collective-permute-start.7
  7.0 10.0 %all-to-all-start = ((bf16[16,2,128,128]{3,2,1,0:T(8,128)(2,1)}), bf16[16,2,128,128]{3,2,1,0:T(8,128)(2,1)S(1)}, u32[]{:S(2)}, u32[]{:S(2)}) async-start(bf16[16,2,128,128]{3,2,1,0:T(8,128)(2,1)} %shard_map.131), calls=%async_computation | async-start | bytes 2097152 | tf_op jit(solution)/shard_map/all_to_all | solution.py:325
  17.0 1.0 collective-permute-start.6
  18.0 0.1 collective-permute-start.1
  18.1 0.1 copy.22
  18.2 0.1 copy.23
  18.3 3.2 %collective-permute-start.2 = (bf16[64,2048]{1,0:T(8,128)(2,1)}, bf16[64,2048]{1,0:T(8,128)(2,1)S(1)}, u32[]{:S(2)}, u32[]{:S(2)}) collective-permute-start(bf16[64,2048]{1,0:T(8,128)(2,1)} %maximum_select_fusion.1), channel_id=1, source_target_pairs={{0,0},{1,8},{2,2},{3,10},{4,4},{5,12},{6,6},{7,14},{8,9},{9,1},{10... | collective-permute-start | bytes 786440 | tf_op jit(solution)/shard_map/ppermute | solution.py:329
  21.5 1.1 collective-permute-start.3
  22.6 0.1 pad_maximum_fusion.1
  22.7 0.1 collective-permute-start.9
  22.9 1.1 collective-permute-done.9
  24.0 0.2 collective-permute-start.8
  24.2 1.0 collective-permute-done.8.rate_other_ref
  25.2 0.2 collective-permute-start.22
  25.4 0.7 collective-permute-done.2.first_ref
  26.0 8.8 %collective-permute-start.4 = (bf16[64,2048]{1,0:T(8,128)(2,1)}, bf16[64,2048]{1,0:T(8,128)(2,1)S(1)}, u32[]{:S(2)}, u32[]{:S(2)}) collective-permute-start(bf16[64,2048]{1,0:T(8,128)(2,1)} %maximum_select_fusion.1), channel_id=1, source_target_pairs={{0,4},{1,12},{2,6},{3,14},{4,0},{5,8},{6,2},{7,10},{8,13},{9,5},{1... | collective-permute-start | bytes 786440 | tf_op jit(solution)/shard_map/ppermute | solution.py:329
  34.9 0.1 maximum_select_fusion.2
  35.0 4.1 %collective-permute-done.4.third_ref = bf16[64,2048]{1,0:T(8,128)(2,1)S(1)} collective-permute-done((bf16[64,2048]{1,0:T(8,128)(2,1)}, bf16[64,2048]{1,0:T(8,128)(2,1)S(1)}, u32[]{:S(2)}, u32[]{:S(2)}) %collective-permute-start.4) | collective-permute-done | bytes 262176 | tf_op jit(solution)/shard_map/ppermute | solution.py:329
  39.1 7.2 %collective-permute-done.5.fourth_ref = bf16[64,2048]{1,0:T(8,128)(2,1)S(1)} collective-permute-done((bf16[64,2048]{1,0:T(8,128)(2,1)}, bf16[64,2048]{1,0:T(8,128)(2,1)S(1)}, u32[]{:S(2)}, u32[]{:S(2)}) %collective-permute-start.5) | collective-permute-done | bytes 262176 | tf_op jit(solution)/shard_map/ppermute | solution.py:329
  46.3 1.2 copy-done.2
  47.5 11.4 %shard_map.132 = (f32[4,4,128,128]{3,2,1,0:T(8,128)}, f32[4,4,128,128]{3,2,1,0:T(8,128)}, f32[4,4,64,128]{3,2,1,0:T(8,128)}, f32[4,4,1,128]{3,2,1,0:T(1,128)}, f32[256,512]{1,0:T(8,128)}) custom-call(f32[2]{0:T(128)S(1)} %copy-done.4, f32[2]{0:T(128)S(1)} %collective-permute-done.1.decay_other_ref, bf16[64,2048]{1,0:T(8,128)(2,1)S(1)} %collective-permute-done.2.first_ref, ...), custom_call_target="tpu_custom_call" | custom-call | tf_op jit(solution)/shard_map/pallas_call | solution.py:354
  58.9 0.1 collective-permute-start.10
  59.0 2.6 %collective-permute-done.10.sent_ref = bf16[16,2,128,128]{3,2,1,0:T(8,128)(2,1)S(1)} collective-permute-done((bf16[16,2,128,128]{3,2,1,0:T(8,128)(2,1)S(1)}, bf16[16,2,128,128]{3,2,1,0:T(8,128)(2,1)S(1)}, u32[]{:S(2)}, u32[]{:S(2)}) %collective-permute-start.10) | collective-permute-done | bytes 1048608 | tf_op jit(solution)/shard_map/ppermute | solution.py:293
  61.6 4.4 %shard_map.133 = (bf16[64,2048]{1,0:T(8,128)(2,1)S(1)}, bf16[64,2048]{1,0:T(8,128)(2,1)S(1)}, bf16[64,2048]{1,0:T(8,128)(2,1)S(1)}, bf16[64,2048]{1,0:T(8,128)(2...) custom-call(s32[128]{0:T(128)S(1)} %copy-done.3, f32[256,512]{1,0:T(8,128)} %get-tuple-element.29.gate_ref, ...), custom_call_target="tpu_custom_call" | custom-call | tf_op jit(solution)/shard_map/pallas_call | solution.py:377
  66.0 4.4 %collective-permute-start.12 = (bf16[64,2048]{1,0:T(8,128)(2,1)S(1)}, bf16[64,2048]{1,0:T(8,128)(2,1)S(1)}, u32[]{:S(2)}, u32[]{:S(2)}) collective-permute-start(bf16[64,2048]{1,0:T(8,128)(2,1)S(1)} %get-tuple-element.37), channel_id=1, source_target_pairs={{0,0},{8,1},{2,2},{10,3},{4,4},{12,5},{6,6},{14,7},{9,8},{1,9},{11... | collective-permute-start | bytes 786440 | tf_op jit(solution)/shard_map/ppermute | solution.py:395
  70.5 2.7 %collective-permute-start.13 = (bf16[64,2048]{1,0:T(8,128)(2,1)S(1)}, bf16[64,2048]{1,0:T(8,128)(2,1)S(1)}, u32[]{:S(2)}, u32[]{:S(2)}) collective-permute-start(bf16[64,2048]{1,0:T(8,128)(2,1)S(1)} %get-tuple-element.38), channel_id=1, source_target_pairs={{2,0},{10,1},{4,2},{12,3},{6,4},{14,5},{0,6},{8,7},{11,8},{3,9},{1... | collective-permute-start | bytes 786440 | tf_op jit(solution)/shard_map/ppermute | solution.py:395
  73.1 0.4 collective-permute-start.14
  73.5 1.9 %collective-permute-start.15 = (bf16[64,2048]{1,0:T(8,128)(2,1)S(1)}, bf16[64,2048]{1,0:T(8,128)(2,1)S(1)}, u32[]{:S(2)}, u32[]{:S(2)}) collective-permute-start(bf16[64,2048]{1,0:T(8,128)(2,1)S(1)} %get-tuple-element.40), channel_id=1, source_target_pairs={{6,0},{14,1},{0,2},{8,3},{2,4},{10,5},{4,6},{12,7},{15,8},{7,9},{9... | collective-permute-start | bytes 786440 | tf_op jit(solution)/shard_map/ppermute | solution.py:395
  75.3 0.0 collective-permute-done.12
  75.4 7.3 %collective-permute-done.13 = bf16[64,2048]{1,0:T(8,128)(2,1)S(1)} collective-permute-done((bf16[64,2048]{1,0:T(8,128)(2,1)S(1)}, bf16[64,2048]{1,0:T(8,128)(2,1)S(1)}, u32[]{:S(2)}, u32[]{:S(2)}) %collective-permute-start.13) | collective-permute-done | bytes 262176 | tf_op jit(solution)/shard_map/ppermute | solution.py:395
  82.7 1.5 %collective-permute-done.14 = bf16[64,2048]{1,0:T(8,128)(2,1)S(1)} collective-permute-done((bf16[64,2048]{1,0:T(8,128)(2,1)S(1)}, bf16[64,2048]{1,0:T(8,128)(2,1)S(1)}, u32[]{:S(2)}, u32[]{:S(2)}) %collective-permute-start.14) | collective-permute-done | bytes 262176 | tf_op jit(solution)/shard_map/ppermute | solution.py:395
  84.2 5.2 %collective-permute-done.15 = bf16[64,2048]{1,0:T(8,128)(2,1)S(1)} collective-permute-done((bf16[64,2048]{1,0:T(8,128)(2,1)S(1)}, bf16[64,2048]{1,0:T(8,128)(2,1)S(1)}, u32[]{:S(2)}, u32[]{:S(2)}) %collective-permute-start.15) | collective-permute-done | bytes 262176 | tf_op jit(solution)/shard_map/ppermute | solution.py:395
  89.4 0.1 fusion.2
  89.5 0.1 collective-permute-start.16
  89.6 0.5 collective-permute-start.23
  90.1 0.3 collective-permute-start.18
  90.4 0.7 collective-permute-done.16
  91.1 0.3 multiply_reduce_fusion
  91.5 0.1 multiply_convert_fusion
  91.6 2.9 %collective-permute-start.17 = (bf16[64,2176]{1,0:T(8,128)(2,1)S(1)}, bf16[64,2176]{1,0:T(8,128)(2,1)S(1)}, u32[]{:S(2)}, u32[]{:S(2)}) collective-permute-start(bf16[64,2176]{1,0:T(8,128)(2,1)S(1)} %pad_maximum_fusion), channel_id=1, source_target_pairs={{0,0},{1,8},{2,2},{3,10},{4,4},{5,12},{6,6},{7,14},{8,9},{9,1},{10... | collective-permute-start | bytes 835592 | tf_op jit(solution)/shard_map/ppermute | solution.py:301
  94.5 0.1 collective-permute-start.19
  94.6 0.3 collective-permute-done.18
  94.9 2.5 %collective-permute-start.20 = (bf16[64,2176]{1,0:T(8,128)(2,1)S(1)}, bf16[64,2176]{1,0:T(8,128)(2,1)S(1)}, u32[]{:S(2)}, u32[]{:S(2)}) collective-permute-start(bf16[64,2176]{1,0:T(8,128)(2,1)S(1)} %pad_maximum_fusion), channel_id=1, source_target_pairs={{0,4},{1,12},{2,6},{3,14},{4,0},{5,8},{6,2},{7,10},{8,13},{9,5},{1... | collective-permute-start | bytes 835592 | tf_op jit(solution)/shard_map/ppermute | solution.py:301
  97.4 2.0 %collective-permute-done.17.first_ref = bf16[64,2176]{1,0:T(8,128)(2,1)S(1)} collective-permute-done((bf16[64,2176]{1,0:T(8,128)(2,1)S(1)}, bf16[64,2176]{1,0:T(8,128)(2,1)S(1)}, u32[]{:S(2)}, u32[]{:S(2)}) %collective-permute-start.17) | collective-permute-done | bytes 278560 | tf_op jit(solution)/shard_map/ppermute | solution.py:301
  99.4 2.9 %collective-permute-start.21 = (bf16[64,2176]{1,0:T(8,128)(2,1)S(1)}, bf16[64,2176]{1,0:T(8,128)(2,1)S(1)}, u32[]{:S(2)}, u32[]{:S(2)}) collective-permute-start(bf16[64,2176]{1,0:T(8,128)(2,1)S(1)} %pad_maximum_fusion), channel_id=1, source_target_pairs={{0,6},{1,14},{2,0},{3,8},{4,2},{5,10},{6,4},{7,12},{8,15},{9,7},{1... | collective-permute-start | bytes 835592 | tf_op jit(solution)/shard_map/ppermute | solution.py:301
  102.2 1.1 maximum_select_fusion
  103.3 7.7 %collective-permute-done.19.second_ref = bf16[64,2176]{1,0:T(8,128)(2,1)S(1)} collective-permute-done((bf16[64,2176]{1,0:T(8,128)(2,1)S(1)}, bf16[64,2176]{1,0:T(8,128)(2,1)S(1)}, u32[]{:S(2)}, u32[]{:S(2)}) %collective-permute-start.19) | collective-permute-done | bytes 278560 | tf_op jit(solution)/shard_map/ppermute | solution.py:301
  111.0 6.5 %shard_map.134 = (bf16[64,2048]{1,0:T(8,128)(2,1)S(1)}, bf16[64,2048]{1,0:T(8,128)(2,1)S(1)}, bf16[64,2048]{1,0:T(8,128)(2,1)S(1)}, bf16[64,2048]{1,0:T(8,128)(2,1)S(1)}) custom-call(s32[1]{0:T(128)} %bitcast.4.mine_ref, bf16[64,2176]{1,0:T(8,128)(2,1)S(1)} %collective-permute-done.17.first_ref, bf16[64,2176]{1,0:T(8,128)(2,1)S(1)} %collective-permute-done.19.second_ref, ...), custom_call_target="tpu_custom_call" | custom-call | tf_op jit(solution)/shard_map/pallas_call | solution.py:409
  117.5 2.8 %collective-permute-start.24 = (bf16[64,2048]{1,0:T(8,128)(2,1)S(1)}, bf16[64,2048]{1,0:T(8,128)(2,1)S(1)}, u32[]{:S(2)}, u32[]{:S(2)}) collective-permute-start(bf16[64,2048]{1,0:T(8,128)(2,1)S(1)} %get-tuple-element.45), channel_id=1, source_target_pairs={{0,0},{8,1},{2,2},{10,3},{4,4},{12,5},{6,6},{14,7},{9,8},{1,9},{11... | collective-permute-start | bytes 786440 | tf_op jit(solution)/shard_map/ppermute | solution.py:395
  120.3 2.1 %collective-permute-start.25 = (bf16[64,2048]{1,0:T(8,128)(2,1)S(1)}, bf16[64,2048]{1,0:T(8,128)(2,1)S(1)}, u32[]{:S(2)}, u32[]{:S(2)}) collective-permute-start(bf16[64,2048]{1,0:T(8,128)(2,1)S(1)} %get-tuple-element.46), channel_id=1, source_target_pairs={{2,0},{10,1},{4,2},{12,3},{6,4},{14,5},{0,6},{8,7},{11,8},{3,9},{1... | collective-permute-start | bytes 786440 | tf_op jit(solution)/shard_map/ppermute | solution.py:395
  122.4 0.9 collective-permute-start.26
  123.3 1.7 %collective-permute-start.27 = (bf16[64,2048]{1,0:T(8,128)(2,1)S(1)}, bf16[64,2048]{1,0:T(8,128)(2,1)S(1)}, u32[]{:S(2)}, u32[]{:S(2)}) collective-permute-start(bf16[64,2048]{1,0:T(8,128)(2,1)S(1)} %get-tuple-element.48), channel_id=1, source_target_pairs={{6,0},{14,1},{0,2},{8,3},{2,4},{10,5},{4,6},{12,7},{15,8},{7,9},{9... | collective-permute-start | bytes 786440 | tf_op jit(solution)/shard_map/ppermute | solution.py:395
  125.0 1.5 %collective-permute-done.24 = bf16[64,2048]{1,0:T(8,128)(2,1)S(1)} collective-permute-done((bf16[64,2048]{1,0:T(8,128)(2,1)S(1)}, bf16[64,2048]{1,0:T(8,128)(2,1)S(1)}, u32[]{:S(2)}, u32[]{:S(2)}) %collective-permute-start.24) | collective-permute-done | bytes 262176 | tf_op jit(solution)/shard_map/ppermute | solution.py:395
  126.5 5.4 %collective-permute-done.25 = bf16[64,2048]{1,0:T(8,128)(2,1)S(1)} collective-permute-done((bf16[64,2048]{1,0:T(8,128)(2,1)S(1)}, bf16[64,2048]{1,0:T(8,128)(2,1)S(1)}, u32[]{:S(2)}, u32[]{:S(2)}) %collective-permute-start.25) | collective-permute-done | bytes 262176 | tf_op jit(solution)/shard_map/ppermute | solution.py:395
  131.9 1.4 collective-permute-done.26
  133.3 5.6 %collective-permute-done.27 = bf16[64,2048]{1,0:T(8,128)(2,1)S(1)} collective-permute-done((bf16[64,2048]{1,0:T(8,128)(2,1)S(1)}, bf16[64,2048]{1,0:T(8,128)(2,1)S(1)}, u32[]{:S(2)}, u32[]{:S(2)}) %collective-permute-start.27) | collective-permute-done | bytes 262176 | tf_op jit(solution)/shard_map/ppermute | solution.py:395
  138.9 0.1 convert_add_fusion
  139.1 0.1 collective-permute-start.28
  139.2 1.3 collective-permute-done.28
  140.5 0.7 fusion.1
  (41 shorter events, 0.2 us)
Async XLA Ops:
  0.6 3.6 %copy-start.6 = (bf16[32,2048]{1,0:T(8,128)(2,1)S(1)}, bf16[32,2048]{1,0:T(8,128)(2,1)}, u32[]{:S(2)}) copy-start(bf16[32,2048]{1,0:T(8,128)(2,1)} %param.12) | copy-start | bytes 393220
  0.6 3.5 %collective-permute-start = (bf16[32,2048]{1,0:T(8,128)(2,1)}, bf16[32,2048]{1,0:T(8,128)(2,1)S(1)}, u32[]{:S(2)}, u32[]{:S(2)}) collective-permute-start(bf16[32,2048]{1,0:T(8,128)(2,1)} %param.12), channel_id=1, source_target_pairs={{0,1},{1,0},{2,3},{3,2},{4,5},{5,4},{6,7},{7,6},{8,9},{9,8},{10,11... | collective-permute-start | bytes 393224 | tf_op jit(solution)/shard_map/ppermute | solution.py:293
  6.8 11.2 %copy-start.4 = (f32[2]{0:T(128)S(1)}, f32[2]{0:T(128)}, u32[]{:S(2)}) copy-start(f32[2]{0:T(128)} %decay_own_ref.1) | copy-start | bytes 28
  6.8 11.3 %copy-start.8 = (f32[32,10]{0,1:T(8,128)S(1)}, f32[32,10]{0,1:T(8,128)}, u32[]{:S(2)}) copy-start(f32[32,10]{0,1:T(8,128)} %param.21) | copy-start | bytes 3844
  6.8 11.3 %copy-start.9 = (s32[32,10]{0,1:T(8,128)S(1)}, s32[32,10]{0,1:T(8,128)}, u32[]{:S(2)}) copy-start(s32[32,10]{0,1:T(8,128)} %param.20) | copy-start | bytes 3844
  6.9 16.0 %copy-start.7 = (bf16[2048,2,2]{0,2,1:T(2,128)(2,1)S(1)}, bf16[2048,2,2]{0,2,1:T(2,128)(2,1)}, u32[]{:S(2)}) copy-start(bf16[2048,2,2]{0,2,1:T(2,128)(2,1)} %param.15) | copy-start | bytes 49156
  6.9 39.4 %collective-permute-start.7 = (bf16[2,2048,256]{2,1,0:T(8,128)(2,1)S(1)}, bf16[2,2048,256]{2,1,0:T(8,128)(2,1)}, u32[]{:S(2)}, u32[]{:S(2)}) collective-permute-start(bf16[2,2048,256]{2,1,0:T(8,128)(2,1)S(1)} %bitcast.9), channel_id=1, source_target_pairs={{0,1},{1,0},{2,3},{3,2},{4,5},{5,4},{6,7},{7,6},{8,9},{9,8},{10,11... | collective-permute-start | bytes 6291464 | tf_op jit(solution)/shard_map/ppermute | solution.py:293
  7.0 51.9 %all-to-all-start = ((bf16[16,2,128,128]{3,2,1,0:T(8,128)(2,1)}), bf16[16,2,128,128]{3,2,1,0:T(8,128)(2,1)S(1)}, u32[]{:S(2)}, u32[]{:S(2)}) async-start(bf16[16,2,128,128]{3,2,1,0:T(8,128)(2,1)} %shard_map.131), calls=%async_computation | async-start | bytes 2097152 | tf_op jit(solution)/shard_map/all_to_all | solution.py:325
  17.0 29.3 %collective-permute-start.6 = (bf16[2048,256]{1,0:T(8,128)(2,1)}, bf16[2048,256]{1,0:T(8,128)(2,1)}, u32[]{:S(2)}, u32[]{:S(2)}) collective-permute-start(bf16[2048,256]{1,0:T(8,128)(2,1)} %bitcast.15), channel_id=1, source_target_pairs={{0,1},{1,0},{2,3},{3,2},{4,5},{5,4},{6,7},{7,6},{8,9},{9,8},{10,11... | collective-permute-start | bytes 3145736 | tf_op jit(solution)/shard_map/ppermute | solution.py:293
  18.0 4.7 %collective-permute-start.1 = (f32[2]{0:T(128)S(1)}, f32[2]{0:T(128)S(1)}, u32[]{:S(2)}, u32[]{:S(2)}) collective-permute-start(f32[2]{0:T(128)S(1)} %copy-done.4), channel_id=1, source_target_pairs={{0,1},{1,0},{2,3},{3,2},{4,5},{5,4},{6,7},{7,6},{8,9},{9,8},{10,11... | collective-permute-start | bytes 32 | tf_op jit(solution)/shard_map/ppermute | solution.py:293
  18.3 7.7 %collective-permute-start.2 = (bf16[64,2048]{1,0:T(8,128)(2,1)}, bf16[64,2048]{1,0:T(8,128)(2,1)S(1)}, u32[]{:S(2)}, u32[]{:S(2)}) collective-permute-start(bf16[64,2048]{1,0:T(8,128)(2,1)} %maximum_select_fusion.1), channel_id=1, source_target_pairs={{0,0},{1,8},{2,2},{3,10},{4,4},{5,12},{6,6},{7,14},{8,9},{9,1},{10... | collective-permute-start | bytes 786440 | tf_op jit(solution)/shard_map/ppermute | solution.py:329
  21.5 13.4 %collective-permute-start.3 = (bf16[64,2048]{1,0:T(8,128)(2,1)}, bf16[64,2048]{1,0:T(8,128)(2,1)}, u32[]{:S(2)}, u32[]{:S(2)}) collective-permute-start(bf16[64,2048]{1,0:T(8,128)(2,1)} %maximum_select_fusion.1), channel_id=1, source_target_pairs={{0,2},{1,10},{2,4},{3,12},{4,6},{5,14},{6,0},{7,8},{8,11},{9,3},{1... | collective-permute-start | bytes 786440 | tf_op jit(solution)/shard_map/ppermute | solution.py:329
  22.7 1.3 collective-permute-start.9
  24.0 1.2 collective-permute-start.8
  25.2 85.8 %collective-permute-start.22 = (bf16[2048,1024]{1,0:T(8,128)(2,1)}, bf16[2048,1024]{1,0:T(8,128)(2,1)}, u32[]{:S(2)}, u32[]{:S(2)}) collective-permute-start(bf16[2048,1024]{1,0:T(8,128)(2,1)} %bitcast.11), channel_id=1, source_target_pairs={{0,1},{1,0},{2,3},{3,2},{4,5},{5,4},{6,7},{7,6},{8,9},{9,8},{10,11... | collective-permute-start | bytes 12582920 | tf_op jit(solution)/shard_map/ppermute | solution.py:293
  26.0 13.0 %collective-permute-start.4 = (bf16[64,2048]{1,0:T(8,128)(2,1)}, bf16[64,2048]{1,0:T(8,128)(2,1)S(1)}, u32[]{:S(2)}, u32[]{:S(2)}) collective-permute-start(bf16[64,2048]{1,0:T(8,128)(2,1)} %maximum_select_fusion.1), channel_id=1, source_target_pairs={{0,4},{1,12},{2,6},{3,14},{4,0},{5,8},{6,2},{7,10},{8,13},{9,5},{1... | collective-permute-start | bytes 786440 | tf_op jit(solution)/shard_map/ppermute | solution.py:329
  34.9 11.4 %collective-permute-start.5 = (bf16[64,2048]{1,0:T(8,128)(2,1)}, bf16[64,2048]{1,0:T(8,128)(2,1)S(1)}, u32[]{:S(2)}, u32[]{:S(2)}) collective-permute-start(bf16[64,2048]{1,0:T(8,128)(2,1)} %maximum_select_fusion.1), channel_id=1, source_target_pairs={{0,6},{1,14},{2,0},{3,8},{4,2},{5,10},{6,4},{7,12},{8,15},{9,7},{1... | collective-permute-start | bytes 786440 | tf_op jit(solution)/shard_map/ppermute | solution.py:329
  39.1 22.6 %copy-start.3 = (s32[128]{0:T(128)S(1)}, s32[128]{0:T(128)}, u32[]{:S(2)}) copy-start(s32[128]{0:T(128)} %resume_ref.3) | copy-start | bytes 1540
  39.1 19.9 %collective-permute-start.11 = (bf16[256,2048]{1,0:T(8,128)(2,1)}, bf16[256,2048]{1,0:T(8,128)(2,1)}, u32[]{:S(2)}, u32[]{:S(2)}) collective-permute-start(bf16[256,2048]{1,0:T(8,128)(2,1)} %bitcast.17), channel_id=1, source_target_pairs={{0,1},{1,0},{2,3},{3,2},{4,5},{5,4},{6,7},{7,6},{8,9},{9,8},{10,11... | collective-permute-start | bytes 3145736 | tf_op jit(solution)/shard_map/ppermute | solution.py:293
  46.3 1.2 copy-start.2
  58.9 2.7 %collective-permute-start.10 = (bf16[16,2,128,128]{3,2,1,0:T(8,128)(2,1)S(1)}, bf16[16,2,128,128]{3,2,1,0:T(8,128)(2,1)S(1)}, u32[]{:S(2)}, u32[]{:S(2)}) collective-permute-start(bf16[16,2,128,128]{3,2,1,0:T(8,128)(2,1)S(1)} %all-to-all-done.held_ref), channel_id=1, source_target_pairs={{0,1},{1,0},{2,3},{3,2},{4,5},{5,4},{6,7},{7,6},{8,9},{9,8},{10,11... | collective-permute-start | bytes 3145736 | tf_op jit(solution)/shard_map/ppermute | solution.py:293
  61.6 28.0 %copy-start.1 = (bf16[1,512,2048]{2,1,0:T(8,128)(2,1)S(1)}, bf16[1,512,2048]{2,1,0:T(8,128)(2,1)}, u32[]{:S(2)}) copy-start(bf16[1,512,2048]{2,1,0:T(8,128)(2,1)} %param.23) | copy-start | bytes 6291460
  61.6 29.5 %copy-start.5 = (bf16[64,2048]{1,0:T(8,128)(2,1)S(1)}, bf16[64,2048]{1,0:T(8,128)(2,1)}, u32[]{:S(2)}) copy-start(bf16[64,2048]{1,0:T(8,128)(2,1)} %maximum_select_fusion.1) | copy-start | bytes 786436
  66.0 9.4 %collective-permute-start.12 = (bf16[64,2048]{1,0:T(8,128)(2,1)S(1)}, bf16[64,2048]{1,0:T(8,128)(2,1)S(1)}, u32[]{:S(2)}, u32[]{:S(2)}) collective-permute-start(bf16[64,2048]{1,0:T(8,128)(2,1)S(1)} %get-tuple-element.37), channel_id=1, source_target_pairs={{0,0},{8,1},{2,2},{10,3},{4,4},{12,5},{6,6},{14,7},{9,8},{1,9},{11... | collective-permute-start | bytes 786440 | tf_op jit(solution)/shard_map/ppermute | solution.py:395
  70.5 12.3 %collective-permute-start.13 = (bf16[64,2048]{1,0:T(8,128)(2,1)S(1)}, bf16[64,2048]{1,0:T(8,128)(2,1)S(1)}, u32[]{:S(2)}, u32[]{:S(2)}) collective-permute-start(bf16[64,2048]{1,0:T(8,128)(2,1)S(1)} %get-tuple-element.38), channel_id=1, source_target_pairs={{2,0},{10,1},{4,2},{12,3},{6,4},{14,5},{0,6},{8,7},{11,8},{3,9},{1... | collective-permute-start | bytes 786440 | tf_op jit(solution)/shard_map/ppermute | solution.py:395
  73.1 11.1 %collective-permute-start.14 = (bf16[64,2048]{1,0:T(8,128)(2,1)S(1)}, bf16[64,2048]{1,0:T(8,128)(2,1)S(1)}, u32[]{:S(2)}, u32[]{:S(2)}) collective-permute-start(bf16[64,2048]{1,0:T(8,128)(2,1)S(1)} %get-tuple-element.39), channel_id=1, source_target_pairs={{4,0},{12,1},{6,2},{14,3},{0,4},{8,5},{2,6},{10,7},{13,8},{5,9},{1... | collective-permute-start | bytes 786440 | tf_op jit(solution)/shard_map/ppermute | solution.py:395
  73.5 15.9 %collective-permute-start.15 = (bf16[64,2048]{1,0:T(8,128)(2,1)S(1)}, bf16[64,2048]{1,0:T(8,128)(2,1)S(1)}, u32[]{:S(2)}, u32[]{:S(2)}) collective-permute-start(bf16[64,2048]{1,0:T(8,128)(2,1)S(1)} %get-tuple-element.40), channel_id=1, source_target_pairs={{6,0},{14,1},{0,2},{8,3},{2,4},{10,5},{4,6},{12,7},{15,8},{7,9},{9... | collective-permute-start | bytes 786440 | tf_op jit(solution)/shard_map/ppermute | solution.py:395
  89.5 1.6 %collective-permute-start.16 = (bf16[64,2048]{1,0:T(8,128)(2,1)S(1)}, bf16[64,2048]{1,0:T(8,128)(2,1)S(1)}, u32[]{:S(2)}, u32[]{:S(2)}) collective-permute-start(bf16[64,2048]{1,0:T(8,128)(2,1)S(1)} %fusion.2), channel_id=1, source_target_pairs={{0,1},{1,0},{2,3},{3,2},{4,5},{5,4},{6,7},{7,6},{8,9},{9,8},{10,11... | collective-permute-start | bytes 786440 | tf_op jit(solution)/shard_map/ppermute | solution.py:293
  89.6 13.7 %collective-permute-start.23 = (bf16[512,2048]{1,0:T(8,128)(2,1)S(1)}, bf16[512,2048]{1,0:T(8,128)(2,1)S(1)}, u32[]{:S(2)}, u32[]{:S(2)}) collective-permute-start(bf16[512,2048]{1,0:T(8,128)(2,1)S(1)} %bitcast.13), channel_id=1, source_target_pairs={{0,1},{1,0},{2,3},{3,2},{4,5},{5,4},{6,7},{7,6},{8,9},{9,8},{10,11... | collective-permute-start | bytes 6291464 | tf_op jit(solution)/shard_map/ppermute | solution.py:293
  90.1 4.8 %collective-permute-start.18 = (f32[4,2,128,128]{3,2,1,0:T(8,128)S(1)}, f32[4,2,128,128]{3,2,1,0:T(8,128)S(1)}, u32[]{:S(2)}, u32[]{:S(2)}) collective-permute-start(f32[4,2,128,128]{3,2,1,0:T(8,128)S(1)} %get-tuple-element.43), channel_id=1, source_target_pairs={{0,1},{1,0},{2,3},{3,2},{4,5},{5,4},{6,7},{7,6},{8,9},{9,8},{10,11... | collective-permute-start | bytes 1572872 | tf_op jit(solution)/shard_map/ppermute | solution.py:293
  91.1 19.9 %copy-start = (bf16[1,2048,1024]{2,1,0:T(8,128)(2,1)S(1)}, bf16[1,2048,1024]{2,1,0:T(8,128)(2,1)}, u32[]{:S(2)}) copy-start(bf16[1,2048,1024]{2,1,0:T(8,128)(2,1)} %param.22) | copy-start | bytes 12582916
  91.6 7.7 %collective-permute-start.17 = (bf16[64,2176]{1,0:T(8,128)(2,1)S(1)}, bf16[64,2176]{1,0:T(8,128)(2,1)S(1)}, u32[]{:S(2)}, u32[]{:S(2)}) collective-permute-start(bf16[64,2176]{1,0:T(8,128)(2,1)S(1)} %pad_maximum_fusion), channel_id=1, source_target_pairs={{0,0},{1,8},{2,2},{3,10},{4,4},{5,12},{6,6},{7,14},{8,9},{9,1},{10... | collective-permute-start | bytes 835592 | tf_op jit(solution)/shard_map/ppermute | solution.py:301
  94.5 16.5 %collective-permute-start.19 = (bf16[64,2176]{1,0:T(8,128)(2,1)S(1)}, bf16[64,2176]{1,0:T(8,128)(2,1)S(1)}, u32[]{:S(2)}, u32[]{:S(2)}) collective-permute-start(bf16[64,2176]{1,0:T(8,128)(2,1)S(1)} %pad_maximum_fusion), channel_id=1, source_target_pairs={{0,2},{1,10},{2,4},{3,12},{4,6},{5,14},{6,0},{7,8},{8,11},{9,3},{1... | collective-permute-start | bytes 835592 | tf_op jit(solution)/shard_map/ppermute | solution.py:301
  94.9 16.2 %collective-permute-start.20 = (bf16[64,2176]{1,0:T(8,128)(2,1)S(1)}, bf16[64,2176]{1,0:T(8,128)(2,1)S(1)}, u32[]{:S(2)}, u32[]{:S(2)}) collective-permute-start(bf16[64,2176]{1,0:T(8,128)(2,1)S(1)} %pad_maximum_fusion), channel_id=1, source_target_pairs={{0,4},{1,12},{2,6},{3,14},{4,0},{5,8},{6,2},{7,10},{8,13},{9,5},{1... | collective-permute-start | bytes 835592 | tf_op jit(solution)/shard_map/ppermute | solution.py:301
  99.4 11.7 %collective-permute-start.21 = (bf16[64,2176]{1,0:T(8,128)(2,1)S(1)}, bf16[64,2176]{1,0:T(8,128)(2,1)S(1)}, u32[]{:S(2)}, u32[]{:S(2)}) collective-permute-start(bf16[64,2176]{1,0:T(8,128)(2,1)S(1)} %pad_maximum_fusion), channel_id=1, source_target_pairs={{0,6},{1,14},{2,0},{3,8},{4,2},{5,10},{6,4},{7,12},{8,15},{9,7},{1... | collective-permute-start | bytes 835592 | tf_op jit(solution)/shard_map/ppermute | solution.py:301
  117.5 8.9 %collective-permute-start.24 = (bf16[64,2048]{1,0:T(8,128)(2,1)S(1)}, bf16[64,2048]{1,0:T(8,128)(2,1)S(1)}, u32[]{:S(2)}, u32[]{:S(2)}) collective-permute-start(bf16[64,2048]{1,0:T(8,128)(2,1)S(1)} %get-tuple-element.45), channel_id=1, source_target_pairs={{0,0},{8,1},{2,2},{10,3},{4,4},{12,5},{6,6},{14,7},{9,8},{1,9},{11... | collective-permute-start | bytes 786440 | tf_op jit(solution)/shard_map/ppermute | solution.py:395
  120.3 11.6 %collective-permute-start.25 = (bf16[64,2048]{1,0:T(8,128)(2,1)S(1)}, bf16[64,2048]{1,0:T(8,128)(2,1)S(1)}, u32[]{:S(2)}, u32[]{:S(2)}) collective-permute-start(bf16[64,2048]{1,0:T(8,128)(2,1)S(1)} %get-tuple-element.46), channel_id=1, source_target_pairs={{2,0},{10,1},{4,2},{12,3},{6,4},{14,5},{0,6},{8,7},{11,8},{3,9},{1... | collective-permute-start | bytes 786440 | tf_op jit(solution)/shard_map/ppermute | solution.py:395
  122.4 10.9 %collective-permute-start.26 = (bf16[64,2048]{1,0:T(8,128)(2,1)S(1)}, bf16[64,2048]{1,0:T(8,128)(2,1)S(1)}, u32[]{:S(2)}, u32[]{:S(2)}) collective-permute-start(bf16[64,2048]{1,0:T(8,128)(2,1)S(1)} %get-tuple-element.47), channel_id=1, source_target_pairs={{4,0},{12,1},{6,2},{14,3},{0,4},{8,5},{2,6},{10,7},{13,8},{5,9},{1... | collective-permute-start | bytes 786440 | tf_op jit(solution)/shard_map/ppermute | solution.py:395
  123.3 15.6 %collective-permute-start.27 = (bf16[64,2048]{1,0:T(8,128)(2,1)S(1)}, bf16[64,2048]{1,0:T(8,128)(2,1)S(1)}, u32[]{:S(2)}, u32[]{:S(2)}) collective-permute-start(bf16[64,2048]{1,0:T(8,128)(2,1)S(1)} %get-tuple-element.48), channel_id=1, source_target_pairs={{6,0},{14,1},{0,2},{8,3},{2,4},{10,5},{4,6},{12,7},{15,8},{7,9},{9... | collective-permute-start | bytes 786440 | tf_op jit(solution)/shard_map/ppermute | solution.py:395
  139.1 1.4 %collective-permute-start.28 = (bf16[32,2048]{1,0:T(8,128)(2,1)S(1)}, bf16[32,2048]{1,0:T(8,128)(2,1)S(1)}, u32[]{:S(2)}, u32[]{:S(2)}) collective-permute-start(bf16[32,2048]{1,0:T(8,128)(2,1)S(1)} %select_convert_fusion), channel_id=1, source_target_pairs={{0,1},{1,0},{2,3},{3,2},{4,5},{5,4},{6,7},{7,6},{8,9},{9,8},{10,11... | collective-permute-start | bytes 393224 | tf_op jit(solution)/shard_map/ppermute | solution.py:293
